TPU v7x, 256 devices: a whole 4x4x8 slice. The times are simulated.
256 devices in a mesh: gx: 8 (over y, x_lo), gy: 2 (over x_hi), vert: 16 (over z, core).
Axes of the slice: x: 4 (x_hi: 2, x_lo: 2; x = x_hi * 2 + x_lo), y: 4, z: 8, core: 2. Of those that a mesh axis runs over, the one named last changes fastest.
Arguments:
- state: float32 [8000, 3, 4, 1024], P('vert', None, 'gy', 'gx'), as said below
- tangent: float32 [8000, 3, 4, 1024], P('vert', None, 'gy', 'gx')
- orient: int32 [8000, 2], P('vert'), may hold values from 0 to 1, as said below
- walls: int32 [2, 1024], P(None, 'gx'), may hold values from 0 to 1
Outputs:
- product: float32 [8000, 3, 4, 1024], P('vert', None, 'gy', 'gx')
Inputs may be any that keep to these rules, and one draw needn't show every extreme that they name: In every aligned group of four slots 4k to 4k+3 there are two bits p, r with orient[4k + 2b + e] = (e XOR p, b XOR r) for b, e in 0, 1. The state's values at the four points q of every cell are positive.
All inputs are finite; a program needn't handle non-finite values.
Results may differ from a plain program's by a relative error of at most 0.0003.
Values sent between devices are 32-bit elements; how exact they have to be, the bound alone decides.
A program may use at most 64 MiB of HBM per device.

v0:
```python
import math

import jax
import jax.numpy as jnp
from jax import lax
from jax.sharding import PartitionSpec as P

NVX = 20


GAUSS = 0.5773502691896258
XI_SIGNS = (-1.0, -1.0, 1.0, 1.0)
ETA_SIGNS = (-1.0, 1.0, -1.0, 1.0)
MIRRORED_DUOS = ((0, 0), (1, 1), (2, 2), (0, 1), (0, 2), (1, 2))
COLLIDE = 2.0
LOG_TWO_PI = math.log(2.0 * math.pi)


def padded(block, sides, width, periodic):
    for axis, dim in sides:
        count = lax.axis_size(axis)
        forward = [(i, i + 1) for i in range(count - 1)]
        if periodic:
            forward.append((count - 1, 0))
        backward = [(target, source) for source, target in forward]
        low = lax.ppermute(
            lax.slice_in_dim(block, block.shape[dim] - width, None, axis=dim), axis, forward
        )
        high = lax.ppermute(lax.slice_in_dim(block, 0, width, axis=dim), axis, backward)
        block = jnp.concatenate([low, block, high], axis=dim)
    return block


def velocities(slot_index, orient, half_grid):
    spacing = 5.0 / half_grid
    mag_x = (slot_index // (4 * half_grid) % half_grid).astype(jnp.float32) + 0.5
    mag_y = (slot_index // 4 % half_grid).astype(jnp.float32) + 0.5
    level_z = (slot_index // (4 * half_grid * half_grid)).astype(jnp.float32) - (half_grid - 0.5)
    sign_x = (2 * orient[:, 0] - 1).astype(jnp.float32)
    sign_y = (2 * orient[:, 1] - 1).astype(jnp.float32)
    return (sign_x * mag_x * spacing, sign_y * mag_y * spacing, level_z * spacing)


def moment_table(vel_x, vel_y, molecular_grid_extent, weight):
    return (
        jnp.stack(
            [
                jnp.ones_like(vel_x),
                vel_x,
                vel_y,
                molecular_grid_extent,
                vel_x * vel_x,
                vel_y * vel_y,
                molecular_grid_extent * molecular_grid_extent,
                vel_x * vel_y,
                vel_x * molecular_grid_extent,
                vel_y * molecular_grid_extent,
            ]
        )
        * weight
    )


def gauss_points(coef):
    center, grad_x, grad_y = (coef[:, 0], coef[:, 1], coef[:, 2])
    return jnp.stack(
        [center + XI_SIGNS[q] * GAUSS * grad_x + ETA_SIGNS[q] * GAUSS * grad_y for q in range(4)],
        axis=1,
    )


def project_points(values):
    total = values[:, 0] + values[:, 1] + values[:, 2] + values[:, 3]
    along_x = values[:, 2] + values[:, 3] - (values[:, 0] + values[:, 1])
    along_y = values[:, 1] + values[:, 3] - (values[:, 0] + values[:, 2])
    return jnp.stack([0.25 * total, 0.75 * GAUSS * along_x, 0.75 * GAUSS * along_y], axis=1)


def partner(values):
    dims_in = values.shape
    grouped = values.reshape((dims_in[0] // 4, 2, 2) + dims_in[1:])
    return grouped[:, ::-1].reshape(dims_in)


def full_matrix(entries):
    rows = [[None, None, None], [None, None, None], [None, None, None]]
    for duo_ordinal, (leading_multiplier, trailing_multiplier) in enumerate(MIRRORED_DUOS):
        rows[leading_multiplier][trailing_multiplier] = entries[duo_ordinal]
        rows[trailing_multiplier][leading_multiplier] = entries[duo_ordinal]
    return rows


def gauss_params(moments):
    density = moments[0]
    average_offset = [moments[1 + leading_multiplier] / density for leading_multiplier in range(3)]
    second = [moments[4 + duo_ordinal] for duo_ordinal in range(6)]
    covariance_array = [
        second[duo_ordinal] / density
        - average_offset[leading_multiplier] * average_offset[trailing_multiplier]
        for duo_ordinal, (leading_multiplier, trailing_multiplier) in enumerate(MIRRORED_DUOS)
    ]
    thermal_state = (covariance_array[0] + covariance_array[1] + covariance_array[2]) / 3.0
    pressure_dyad = [
        (1.5 * thermal_state if leading_multiplier == trailing_multiplier else 0.0)
        - 0.5 * covariance_array[duo_ordinal]
        for duo_ordinal, (leading_multiplier, trailing_multiplier) in enumerate(MIRRORED_DUOS)
    ]
    tens_full = full_matrix(pressure_dyad)
    cofactor = [
        tens_full[1][1] * tens_full[2][2] - tens_full[1][2] * tens_full[1][2],
        tens_full[0][0] * tens_full[2][2] - tens_full[0][2] * tens_full[0][2],
        tens_full[0][0] * tens_full[1][1] - tens_full[0][1] * tens_full[0][1],
        tens_full[0][2] * tens_full[1][2] - tens_full[0][1] * tens_full[2][2],
        tens_full[0][1] * tens_full[1][2] - tens_full[0][2] * tens_full[1][1],
        tens_full[0][1] * tens_full[0][2] - tens_full[0][0] * tens_full[1][2],
    ]
    determinant = (
        tens_full[0][0] * cofactor[0]
        + tens_full[0][1] * cofactor[3]
        + tens_full[0][2] * cofactor[4]
    )
    inverse = [entry / determinant for entry in cofactor]
    log_pre = jnp.log(density) - 1.5 * LOG_TWO_PI - 0.5 * jnp.log(determinant)
    delta_density = moments[10]
    drift_delta = [
        (moments[11 + leading_multiplier] - average_offset[leading_multiplier] * delta_density)
        / density
        for leading_multiplier in range(3)
    ]
    dtheta = [
        moments[14 + duo_ordinal] / density
        - second[duo_ordinal] * delta_density / (density * density)
        - (
            drift_delta[leading_multiplier] * average_offset[trailing_multiplier]
            + average_offset[leading_multiplier] * drift_delta[trailing_multiplier]
        )
        for duo_ordinal, (leading_multiplier, trailing_multiplier) in enumerate(MIRRORED_DUOS)
    ]
    temp_delta = (dtheta[0] + dtheta[1] + dtheta[2]) / 3.0
    tens_delta = [
        (1.5 * temp_delta if leading_multiplier == trailing_multiplier else 0.0)
        - 0.5 * dtheta[duo_ordinal]
        for duo_ordinal, (leading_multiplier, trailing_multiplier) in enumerate(MIRRORED_DUOS)
    ]
    inv_full = full_matrix(inverse)
    delta_full = full_matrix(tens_delta)
    trace_term = sum(
        [
            inv_full[leading_multiplier][trailing_multiplier]
            * delta_full[trailing_multiplier][leading_multiplier]
            for leading_multiplier in range(3)
            for trailing_multiplier in range(3)
        ]
    )
    shift_term = delta_density / density - 0.5 * trace_term
    weight_vec = [
        inv_full[leading_multiplier][0] * drift_delta[0]
        + inv_full[leading_multiplier][1] * drift_delta[1]
        + inv_full[leading_multiplier][2] * drift_delta[2]
        for leading_multiplier in range(3)
    ]
    inner_prod = [
        [
            inv_full[leading_multiplier][0] * delta_full[0][c]
            + inv_full[leading_multiplier][1] * delta_full[1][c]
            + inv_full[leading_multiplier][2] * delta_full[2][c]
            for c in range(3)
        ]
        for leading_multiplier in range(3)
    ]
    curve_sym = [
        inner_prod[leading_multiplier][0] * inv_full[0][trailing_multiplier]
        + inner_prod[leading_multiplier][1] * inv_full[1][trailing_multiplier]
        + inner_prod[leading_multiplier][2] * inv_full[2][trailing_multiplier]
        for leading_multiplier, trailing_multiplier in MIRRORED_DUOS
    ]
    return jnp.stack(average_offset + inverse + [log_pre, shift_term] + weight_vec + curve_sym)


def quadratic(entries, rel_x, rel_y, rel_z):
    return (
        entries[0] * rel_x * rel_x
        + entries[1] * rel_y * rel_y
        + entries[2] * rel_z * rel_z
        + 2.0
        * (entries[3] * rel_x * rel_y + entries[4] * rel_x * rel_z + entries[5] * rel_y * rel_z)
    )


def gauss_tangent(vel_x, vel_y, molecular_grid_extent, params):
    rel_x = vel_x[:, None] - params[0]
    rel_y = vel_y[:, None] - params[1]
    rel_z = molecular_grid_extent[:, None] - params[2]
    gauss = jnp.exp(params[9] - 0.5 * quadratic(params[3:9], rel_x, rel_y, rel_z))
    return gauss * (
        params[10]
        + rel_x * params[11]
        + rel_y * params[12]
        + rel_z * params[13]
        + 0.5 * quadratic(params[14:20], rel_x, rel_y, rel_z)
    )


def transport(coef, orient, vel_x, vel_y, left_in, right_in, below_in, above_in):
    center, grad_x, grad_y = (coef[:, 0], coef[:, 1], coef[:, 2])
    heads_right = (orient[:, 0] == 1)[:, None, None]
    heads_up = (orient[:, 1] == 1)[:, None, None]
    right_val = jnp.where(heads_right, center + grad_x, right_in[0])
    right_slope = jnp.where(heads_right, grad_y, right_in[1])
    left_val = jnp.where(heads_right, left_in[0], center - grad_x)
    left_slope = jnp.where(heads_right, left_in[1], grad_y)
    top_val = jnp.where(heads_up, center + grad_y, above_in[0])
    top_slope = jnp.where(heads_up, grad_x, above_in[1])
    bottom_val = jnp.where(heads_up, below_in[0], center - grad_y)
    bottom_slope = jnp.where(heads_up, below_in[1], grad_x)
    speed_x = vel_x[:, None, None]
    speed_y = vel_y[:, None, None]
    rate_mean = speed_x * (right_val - left_val) + speed_y * (top_val - bottom_val)
    rate_x = 3.0 * speed_x * (right_val + left_val - 2.0 * center) + speed_y * (
        top_slope - bottom_slope
    )
    rate_y = speed_x * (right_slope - left_slope) + 3.0 * speed_y * (
        top_val + bottom_val - 2.0 * center
    )
    return jnp.stack([rate_mean, rate_x, rate_y], axis=1)


def shards(state, tangent, orient, walls):
    slots_here = state.shape[0]
    cell_rows = state.shape[2]
    cell_cols = state.shape[3]
    half_grid = NVX // 2
    weight = (5.0 / half_grid) ** 3
    point_count = 4 * cell_rows * cell_cols
    slot_index = lax.axis_index("vert") * slots_here + jnp.arange(slots_here, dtype=jnp.int32)
    vel_x, vel_y, molecular_grid_extent = velocities(slot_index, orient, half_grid)
    moment_rows = moment_table(vel_x, vel_y, molecular_grid_extent, weight)
    stacked = jnp.concatenate(
        [
            gauss_points(state).reshape(slots_here, point_count),
            gauss_points(tangent).reshape(slots_here, point_count),
        ],
        axis=1,
    )
    partial_sums = jnp.dot(
        moment_rows, stacked, precision=lax.Precision.HIGHEST, preferred_element_type=jnp.float32
    )
    partial_sums = jnp.concatenate(
        [partial_sums[:, :point_count], partial_sums[:, point_count:]], axis=0
    )
    params = gauss_params(lax.psum(partial_sums, "vert"))
    center, grad_x, grad_y = (tangent[:, 0], tangent[:, 1], tangent[:, 2])
    x_padded = padded(tangent, (("gx", 3),), 1, True)
    western = x_padded[:, :, :, :-2]
    eastern = x_padded[:, :, :, 2:]
    left_in = (western[:, 0] + western[:, 1], western[:, 2])
    right_in = (eastern[:, 0] - eastern[:, 1], eastern[:, 2])
    y_padded = padded(tangent, (("gy", 2),), 1, False)
    southern = y_padded[:, :, :-2]
    northern = y_padded[:, :, 2:]
    below_in = (southern[:, 0] + southern[:, 2], southern[:, 1])
    above_in = (northern[:, 0] - northern[:, 2], northern[:, 1])
    floor_flag = walls[0].astype(jnp.float32)
    roof_flag = walls[1].astype(jnp.float32)
    at_bottom = lax.axis_index("gy") == 0
    at_top = lax.axis_index("gy") == lax.axis_size("gy") - 1
    floor_val = (floor_flag * partner(center - grad_y)[:, 0], floor_flag * partner(grad_x)[:, 0])
    roof_val = (roof_flag * partner(center + grad_y)[:, -1], roof_flag * partner(grad_x)[:, -1])
    below_in = tuple(
        (
            jnp.concatenate(
                [jnp.where(at_bottom, wall_part, field_part[:, 0])[:, None], field_part[:, 1:]],
                axis=1,
            )
            for field_part, wall_part in zip(below_in, floor_val)
        )
    )
    above_in = tuple(
        (
            jnp.concatenate(
                [field_part[:, :-1], jnp.where(at_top, wall_part, field_part[:, -1])[:, None]],
                axis=1,
            )
            for field_part, wall_part in zip(above_in, roof_val)
        )
    )
    advected = transport(tangent, orient, vel_x, vel_y, left_in, right_in, below_in, above_in)
    gauss_delta = gauss_tangent(vel_x, vel_y, molecular_grid_extent, params).reshape(
        slots_here, 4, cell_rows, cell_cols
    )
    return advected + COLLIDE * (tangent - project_points(gauss_delta))


def solution(mesh):
    placed = (
        P("vert", None, "gy", "gx"),
        P("vert", None, "gy", "gx"),
        P("vert", None),
        P(None, "gx"),
    )
    return jax.shard_map(
        shards, mesh=mesh, in_specs=placed, out_specs=P("vert", None, "gy", "gx"), check_vma=False
    )
```

profile of v0, /device:TPU:1, one launch (start us, length us, event | category | flops | bytes accessed | tf_op | source)
XLA Modules:
  0.0 193.0 jit_solution(14825529700817234752)
XLA Ops:
  7.5 2.6 %multiply_add_fusion.9 = (f32[500,1,2,128]{3,2,1,0:T(2,128)S(1)}, f32[500,1,2,128]{3,2,1,0:T(2,128)S(1)}, f32[500,1,2,128]{3,2,1,0:T(2,128)S(1)}, f32[500,1,2,12...) fusion(f32[500,3,2,128]{3,2,1,0:T(2,128)} %param.5), kind=kLoop, calls=%fused_computation.98 | loop fusion | flops 1536000 | bytes 5120000 | tf_op jit(solution)/shard_map/add | solution.py:67
  10.1 1.9 pad_maximum_fusion.1
  12.0 3.9 %reshape.660 = f32[500,1024]{1,0:T(8,128)} reshape(f32[500,4,2,128]{3,2,1,0:T(2,128)} %pad_maximum_fusion.1) | data formatting | bytes 4096000 | tf_op jit(solution)/shard_map/reshape | solution.py:241
  15.8 2.3 %multiply_add_fusion.13 = (f32[500,1,2,128]{3,2,1,0:T(2,128)S(1)}, f32[500,1,2,128]{3,2,1,0:T(2,128)S(1)}, f32[500,1,2,128]{3,2,1,0:T(2,128)S(1)}, f32[500,1,2,128]{3,2,1,0:T(2,128)S(1)}) fusion(f32[500,3,2,128]{3,2,1,0:T(2,128)} %param.4), kind=kLoop, calls=%fused_computation.102 | loop fusion | flops 1280000 | bytes 3584000 | tf_op jit(solution)/shard_map/add | solution.py:67
  18.1 1.9 pad_maximum_fusion
  20.0 3.9 %reshape.659 = f32[500,1024]{1,0:T(8,128)} reshape(f32[500,4,2,128]{3,2,1,0:T(2,128)} %pad_maximum_fusion) | data formatting | bytes 4096000 | tf_op jit(solution)/shard_map/reshape | solution.py:240
  24.0 4.4 %fusion = f32[10,2048]{1,0:T(8,128)S(1)} fusion(f32[500,1024]{1,0:T(8,128)} %reshape.660, f32[500,1024]{1,0:T(8,128)} %reshape.659, f32[10,500]{1,0:T(8,128)S(1)} %stack.11), kind=kOutput, calls=%fused_computation.27 | convolution fusion | flops 123909000 | bytes 4197920 | tf_op jit(solution)/shard_map/dot_general | solution.py:245
  29.1 2.3 %fusion.102 = (f32[500,3,1,128]{3,2,0,1:T(1,128)}, f32[500,3,1,128]{3,2,0,1:T(1,128)}) fusion(f32[500,3,2,128]{3,2,1,0:T(2,128)S(1)} %copy-done), kind=kLoop, calls=%fused_computation.265 | loop fusion | bytes 3072000 | tf_op jit(solution)/shard_map/slice | solution.py:29
  32.7 7.3 %collective-permute-start.3 = (f32[500,3,1,128]{3,2,0,1:T(1,128)}, f32[500,3,1,128]{3,2,0,1:T(1,128)}, u32[]{:S(2)}, u32[]{:S(2)}) collective-permute-start(f32[500,3,1,128]{3,2,0,1:T(1,128)} %get-tuple-element.79), channel_id=1, source_target_pairs={{0,16},{1,17},{2,18},{3,19},{4,20},{5,21},{6,22},{7,23},{8,24},{9,... | collective-permute-start | bytes 2304008 | tf_op jit(solution)/shard_map/ppermute | solution.py:26
  40.0 3.8 %fusion.103 = (f32[500,3,2,1]{3,2,1,0:T(2,128)}, f32[500,3,2,1]{3,2,1,0:T(2,128)}) fusion(f32[500,3,2,128]{3,2,1,0:T(2,128)S(1)} %copy-done), kind=kLoop, calls=%fused_computation.266 | loop fusion | bytes 48000 | tf_op jit(solution)/shard_map/slice | solution.py:29
  43.7 2.5 %copy.33 = f32[500,3,2,1]{0,2,3,1:T(2,128)S(1)} copy(f32[500,3,2,1]{3,2,1,0:T(2,128)} %get-tuple-element.80) | data formatting | bytes 24000
  46.2 4.5 %collective-permute-start = (f32[500,3,2,1]{0,2,3,1:T(2,128)S(1)}, f32[500,3,2,1]{0,2,3,1:T(2,128)S(1)}, u32[]{:S(2)}, u32[]{:S(2)}) collective-permute-start(f32[500,3,2,1]{0,2,3,1:T(2,128)S(1)} %copy.33), channel_id=1, source_target_pairs={{32,0},{64,32},{96,64},{128,96},{160,128},{192,160},{224,192},{0,2... | collective-permute-start | bytes 36008 | tf_op jit(solution)/shard_map/ppermute | solution.py:29
  50.7 2.4 %copy.34 = f32[500,3,2,1]{0,2,3,1:T(2,128)S(1)} copy(f32[500,3,2,1]{3,2,1,0:T(2,128)} %get-tuple-element.81) | data formatting | bytes 24000
  56.4 1.6 collective-permute-done
  60.3 2.0 %copy.20 = f32[500,3,2,1]{3,2,1,0:T(2,128)} copy(f32[500,3,2,1]{0,2,3,1:T(2,128)S(1)} %collective-permute-done.1) | data formatting | bytes 24000 | tf_op jit(solution)/shard_map/ppermute | solution.py:26
  62.3 77.0 %all-reduce.2.cloned.1.call-done = f32[20,1024]{1,0:T(8,128)} async-done(((f32[20,1024]{1,0:T(8,128)}), f32[20,1024]{1,0:T(8,128)}) %all-reduce.2.cloned.1.call-update) | async-done | bytes 81936 | tf_op jit(solution)/shard_map/psum | solution.py:251
  143.8 16.4 %fusion.14 = f32[500,4,2,128]{3,2,1,0:T(2,128)S(1)} fusion(f32[4,2,128]{2,1,0:T(2,128)S(1)} %bitcast.102, f32[4,2,128]{2,1,0:T(2,128)S(1)} %bitcast.105, f32[4,2,128]{2,1,0:T(2,128)S(1)} %bitcast.104, f32[4,2,128]{2,1,0:T(2,128)S(1)} %bitcast.103, f32[4,2,128]{2,1,0:T(2,128)S(1)} %bitcast.106, f32[4,2,128]{2,1,0:T(2,128)S(1)} %bitcast.101, ...), kind=kLoop, calls=%fused_computation.41 | loop fusion | flops 25600000 | bytes 2135920 | tf_op jit(solution)/shard_map/mul | solution.py:195
  161.2 4.0 %fusion.31 = (f32[500,2,128]{2,1,0:T(2,128)S(1)}, f32[500,2,128]{2,1,0:T(2,128)S(1)}, f32[500,2,128]{2,1,0:T(2,128)S(1)}, f32[500,2,128]{2,1,0:T(2,128)S(1)}) fusion(f32[500,3,1,128]{3,2,0,1:T(1,128)} %collective-permute-done.3, f32[500,3,1,128]{3,2,0,1:T(1,128)} %collective-permute-done.2, f32[500,3,2,128]{3,2,1,0:T(2,128)S(1)} %copy-done), kind=kLoop, calls=%fused_computation.66 | loop fusion | flops 1024000 | bytes 5120000 | tf_op jit(solution)/shard_map/squeeze | solution.py:261
  165.8 1.4 fusion.40
  168.2 6.2 %multiply_add_fusion.5 = (f32[500,1,2,128]{3,2,1,0:T(2,128)S(1)}, f32[500,1,2,128]{3,2,1,0:T(2,128)S(1)}, f32[500,1,2,128]{3,2,1,0:T(2,128)S(1)}) fusion(f32[500]{0:T(512)S(1)} %get-tuple-element.122, f32[500]{0:T(512)S(1)} %broadcast_multiply_fusion.3, f32[500,1,2,128]{3,2,1,0:T(2,128)S(1)} %bitcast.76, f32[500,1,2,128]{3,2,1,0:T(2,128)S(1)} %copy-done.3, ...), kind=kLoop, calls=%fused_computation.88 | loop fusion | flops 2304000 | bytes 9221120 | tf_op jit(solution)/shard_map/add | solution.py:218
  174.4 4.7 %fusion.29 = f32[500,1,2,128]{3,2,1,0:T(2,128)S(1)} fusion(f32[500,3,2,128]{3,2,1,0:T(2,128)S(1)} %copy-done, f32[500,3,2,1]{3,2,1,0:T(2,128)S(1)} %copy-done.1, f32[500,3,2,1]{3,2,1,0:T(2,128)S(1)} %copy.18, pred[500]{0:T(512)(128)(4,1)S(1)} %get-tuple-element.6, f32[500]{0:T(512)S(1)} %broadcast_multiply_fusion, f32[500]{0:T(512)S(1)} %broadcast_multiply_fusion.3, ...), kind=kLoop, calls=%fused_computation.62 | loop fusion | flops 1792000 | bytes 8197120 | tf_op jit(solution)/shard_map/add | solution.py:222
  179.1 1.8 broadcast_select_fusion
  180.8 2.8 %multiply_add_fusion.4 = f32[500,1,2,128]{3,2,1,0:T(2,128)S(1)} fusion(f32[500,1,2,128]{3,2,1,0:T(2,128)S(1)} %bitcast.82, f32[500,1,2,128]{3,2,1,0:T(2,128)S(1)} %bitcast.81, f32[500,1,2,128]{3,2,1,0:T(2,128)S(1)} %get-tuple-element.53, f32[500,1,2,128]{3,2,1,0:T(2,128)S(1)} %get-tuple-element.52, pred[500]{0:T(512)(128)(4,1)S(1)} %get-tuple-element.5, ...), kind=kLoop, calls=%fused_computation.87 | loop fusion | flops 1024000 | bytes 3588500 | tf_op jit(solution)/shard_map/add | solution.py:219
  183.7 2.5 %maximum_add_fusion = f32[500,3,2,128]{3,2,1,0:T(2,128)} fusion(f32[500,1,2,128]{3,2,1,0:T(2,128)S(1)} %fusion.29, f32[500,1,2,128]{3,2,1,0:T(2,128)S(1)} %multiply_add_fusion.4, f32[500,1,2,128]{3,2,1,0:T(2,128)S(1)} %get-tuple-element.51, f32[500,3,2,128]{3,2,1,0:T(2,128)S(1)} %copy-done, f32[500,1,2,128]{3,2,1,0:T(2,128)S(1)} %get-tuple-element.64, ...), kind=kLoop, calls=%fused_computation.54 | loop fusion | flops 2688000 | bytes 6144000 | tf_op jit(solution)/shard_map/add | solution.py:291
  (61 shorter events, 15.2 us)
Async XLA Ops:
  6.5 132.8 %all-reduce.2.cloned.1.call-start = ((), (), s32[]{:S(2)}) async-start(), calls=%async_computation | async-start | bytes 196608 | tf_op jit(solution)/shard_map/psum | solution.py:251
  10.0 43.4 %copy-start.2 = (f32[500,1,2,128]{3,2,1,0:T(2,128)}, f32[500,1,2,128]{3,2,1,0:T(2,128)S(1)}, u32[]{:S(2)}) copy-start(f32[500,1,2,128]{3,2,1,0:T(2,128)S(1)} %get-tuple-element.73) | copy-start | bytes 1536004
  10.1 44.3 %copy-start.6 = (f32[500,1,2,128]{3,2,1,0:T(2,128)}, f32[500,1,2,128]{3,2,1,0:T(2,128)S(1)}, u32[]{:S(2)}) copy-start(f32[500,1,2,128]{3,2,1,0:T(2,128)S(1)} %get-tuple-element.74) | copy-start | bytes 1536004
  10.1 45.3 %copy-start.4 = (f32[500,1,2,128]{3,2,1,0:T(2,128)}, f32[500,1,2,128]{3,2,1,0:T(2,128)S(1)}, u32[]{:S(2)}) copy-start(f32[500,1,2,128]{3,2,1,0:T(2,128)S(1)} %get-tuple-element.75) | copy-start | bytes 1536004
  24.0 5.1 %copy-start = (f32[500,3,2,128]{3,2,1,0:T(2,128)S(1)}, f32[500,3,2,128]{3,2,1,0:T(2,128)}, u32[]{:S(2)}) copy-start(f32[500,3,2,128]{3,2,1,0:T(2,128)} %param.5) | copy-start | bytes 4608004
  31.4 129.7 %collective-permute-start.2 = (f32[500,3,1,128]{3,2,0,1:T(1,128)}, f32[500,3,1,128]{3,2,0,1:T(1,128)}, u32[]{:S(2)}, u32[]{:S(2)}) collective-permute-start(f32[500,3,1,128]{3,2,0,1:T(1,128)} %get-tuple-element.78), channel_id=1, source_target_pairs={{16,0},{17,1},{18,2},{19,3},{20,4},{21,5},{22,6},{23,7},{24,8},{25... | collective-permute-start | bytes 2304008 | tf_op jit(solution)/shard_map/ppermute | solution.py:29
  32.7 128.5 %collective-permute-start.3 = (f32[500,3,1,128]{3,2,0,1:T(1,128)}, f32[500,3,1,128]{3,2,0,1:T(1,128)}, u32[]{:S(2)}, u32[]{:S(2)}) collective-permute-start(f32[500,3,1,128]{3,2,0,1:T(1,128)} %get-tuple-element.79), channel_id=1, source_target_pairs={{0,16},{1,17},{2,18},{3,19},{4,20},{5,21},{6,22},{7,23},{8,24},{9,... | collective-permute-start | bytes 2304008 | tf_op jit(solution)/shard_map/ppermute | solution.py:26
  43.7 9.6 %copy-start.11 = (s32[500,2]{0,1:T(2,128)S(1)}, s32[500,2]{0,1:T(2,128)}, u32[]{:S(2)}) copy-start(s32[500,2]{0,1:T(2,128)} %param.6) | copy-start | bytes 12004
  43.7 9.6 %copy-start.12 = (s32[2,128]{1,0:T(2,128)S(1)}, s32[2,128]{1,0:T(2,128)}, u32[]{:S(2)}) copy-start(s32[2,128]{1,0:T(2,128)} %param.7) | copy-start | bytes 3076
  46.2 11.8 %collective-permute-start = (f32[500,3,2,1]{0,2,3,1:T(2,128)S(1)}, f32[500,3,2,1]{0,2,3,1:T(2,128)S(1)}, u32[]{:S(2)}, u32[]{:S(2)}) collective-permute-start(f32[500,3,2,1]{0,2,3,1:T(2,128)S(1)} %copy.33), channel_id=1, source_target_pairs={{32,0},{64,32},{96,64},{128,96},{160,128},{192,160},{224,192},{0,2... | collective-permute-start | bytes 36008 | tf_op jit(solution)/shard_map/ppermute | solution.py:29
  53.2 7.1 %collective-permute-start.1 = (f32[500,3,2,1]{0,2,3,1:T(2,128)S(1)}, f32[500,3,2,1]{0,2,3,1:T(2,128)S(1)}, u32[]{:S(2)}, u32[]{:S(2)}) collective-permute-start(f32[500,3,2,1]{0,2,3,1:T(2,128)S(1)} %copy.34), channel_id=1, source_target_pairs={{0,32},{32,64},{64,96},{96,128},{128,160},{160,192},{192,224},{224... | collective-permute-start | bytes 36008 | tf_op jit(solution)/shard_map/ppermute | solution.py:26
  161.1 4.1 %copy-start.10 = (f32[125,2,2,2,128]{4,3,2,1,0:T(2,128)S(1)}, f32[125,2,2,2,128]{4,3,2,1,0:T(2,128)}, u32[]{:S(2)}) copy-start(f32[125,2,2,2,128]{4,3,2,1,0:T(2,128)} %rev.10) | copy-start | bytes 1536004
  161.1 4.6 %copy-start.8 = (f32[125,2,2,2,128]{4,3,2,1,0:T(2,128)S(1)}, f32[125,2,2,2,128]{4,3,2,1,0:T(2,128)}, u32[]{:S(2)}) copy-start(f32[125,2,2,2,128]{4,3,2,1,0:T(2,128)} %rev.12) | copy-start | bytes 1536004
  161.1 4.6 %copy-start.9 = (f32[125,2,2,2,128]{4,3,2,1,0:T(2,128)S(1)}, f32[125,2,2,2,128]{4,3,2,1,0:T(2,128)}, u32[]{:S(2)}) copy-start(f32[125,2,2,2,128]{4,3,2,1,0:T(2,128)} %rev.11) | copy-start | bytes 1536004
  165.8 2.3 %copy-start.1 = (f32[500,3,2,1]{3,2,1,0:T(2,128)S(1)}, f32[500,3,2,1]{3,2,1,0:T(2,128)}, u32[]{:S(2)}) copy-start(f32[500,3,2,1]{3,2,1,0:T(2,128)} %copy.20) | copy-start | bytes 36004
  165.8 2.3 %copy-start.3 = (f32[500,1,2,128]{3,2,1,0:T(2,128)S(1)}, f32[500,1,2,128]{3,2,1,0:T(2,128)}, u32[]{:S(2)}) copy-start(f32[500,1,2,128]{3,2,1,0:T(2,128)} %copy-done.2) | copy-start | bytes 1536004
  165.8 2.3 %copy-start.5 = (f32[500,1,2,128]{3,2,1,0:T(2,128)S(1)}, f32[500,1,2,128]{3,2,1,0:T(2,128)}, u32[]{:S(2)}) copy-start(f32[500,1,2,128]{3,2,1,0:T(2,128)} %copy-done.4) | copy-start | bytes 1536004
  174.4 4.7 %copy-start.7 = (f32[500,1,2,128]{3,2,1,0:T(2,128)S(1)}, f32[500,1,2,128]{3,2,1,0:T(2,128)}, u32[]{:S(2)}) copy-start(f32[500,1,2,128]{3,2,1,0:T(2,128)} %copy-done.6) | copy-start | bytes 1536004
Sparse Core Ops, SparseCore 0:
  29.2 110.0 all-reduce.1
where the time goes:
time: 194 us; the launch traced here: 193 us
  waiting for transfers between devices  79.8 us (41%)
  other arithmetic  56.9 us (29%)
  local copies, waits for them, and re-layouts  25 us (13%)
  between operations  13.8 us (7%)
  starting transfers between devices  13.2 us (7%)
  matrix products  4.37 us (2%)
    psum x1, waiting for transfers between devices, shards(): params = gauss_params(lax.psum(partial_sums, 'vert'))  77 us
    mul x1, other arithmetic, gauss_tangent(): gauss * (params[10] + rel_x * params[11] + rel_y * params[12] + rel_z * p...  16.4 us
    ppermute x2, starting transfers between devices, padded(): lax.ppermute(lax.slice_in_dim(block, block.shape[dim] - width, None, axis...  7.33 us
    add x1, other arithmetic, transport(): speed_x * (right_val - left_val) + speed_y * (top_val - bottom_val)  6.21 us
    slice x2, local copies, waits for them, and re-layouts, padded(): lax.slice_in_dim(block, 0, width, axis=dim)  6.09 us
    ppermute x2, starting transfers between devices, padded(): lax.ppermute(lax.slice_in_dim(block, 0, width, axis=dim), axis, backward)  5.82 us
    unnamed x28, local copies, waits for them, and re-layouts  4.98 us
    add x2, other arithmetic, gauss_points(): center + XI_SIGNS[q] * GAUSS * grad_x + ETA_SIGNS[q] * GAUSS * grad_y  4.89 us
  transfers between devices with their start and end apart: 5, of which 3 were waited for; matrix products, arithmetic and copies ran while one was open for 20% of the time, Pallas kernels for 0%

commit v1 on v0

v1 whole, which is shorter than its diff:
```python
import functools
import math

import jax
import jax.numpy as jnp
from jax import lax
from jax.experimental import pallas as pl
from jax.experimental.pallas import tpu as pltpu
from jax.sharding import PartitionSpec as P

MESH = pl.DeviceIdType.MESH
F32 = jnp.float32
BF16 = jnp.bfloat16

SLOTS = 500
PAD = 512
TILES = PAD // 8
HALF = TILES // 2
ROWS = SLOTS * 6
PAD_ROWS = PAD * 6
GAUSS = 0.5773502691896258
LOG_TWO_PI = math.log(2.0 * math.pi)
LOG2E = math.log2(math.e)
DUOS = ((0, 0), (1, 1), (2, 2), (0, 1), (0, 2), (1, 2))
PEERS = 16
ORDER = (8, 7, 9, 6, 10, 5, 11, 4, 12, 3, 13, 2, 14, 1, 15)


def full(entries):
    rows = [[None] * 3 for _ in range(3)]
    for n, (a, b) in enumerate(DUOS):
        rows[a][b] = entries[n]
        rows[b][a] = entries[n]
    return rows


def gauss_coefs(mom):
    rho = mom[0]
    inv_rho = 1.0 / rho
    u = [mom[1 + a] * inv_rho for a in range(3)]
    sec = mom[4:10]
    theta = [sec[n] * inv_rho - u[a] * u[b] for n, (a, b) in enumerate(DUOS)]
    temp = (theta[0] + theta[1] + theta[2]) * (1.0 / 3.0)
    tn = [(1.5 * temp if a == b else 0.0) - 0.5 * theta[n] for n, (a, b) in enumerate(DUOS)]
    t = full(tn)
    cof = [
        t[1][1] * t[2][2] - t[1][2] * t[1][2],
        t[0][0] * t[2][2] - t[0][2] * t[0][2],
        t[0][0] * t[1][1] - t[0][1] * t[0][1],
        t[0][2] * t[1][2] - t[0][1] * t[2][2],
        t[0][1] * t[1][2] - t[0][2] * t[1][1],
        t[0][1] * t[0][2] - t[0][0] * t[1][2],
    ]
    det = t[0][0] * cof[0] + t[0][1] * cof[3] + t[0][2] * cof[4]
    inv_det = 1.0 / det
    inv = [c * inv_det for c in cof]
    log_pre = jnp.log(rho) - 1.5 * LOG_TWO_PI - 0.5 * jnp.log(det)
    drho = mom[10]
    du = [(mom[11 + a] - u[a] * drho) * inv_rho for a in range(3)]
    dlog = drho * inv_rho
    dtheta = [
        (mom[14 + n] - sec[n] * dlog) * inv_rho - (du[a] * u[b] + u[a] * du[b])
        for n, (a, b) in enumerate(DUOS)
    ]
    dtemp = (dtheta[0] + dtheta[1] + dtheta[2]) * (1.0 / 3.0)
    dtn = [(1.5 * dtemp if a == b else 0.0) - 0.5 * dtheta[n] for n, (a, b) in enumerate(DUOS)]
    A = full(inv)
    D = full(dtn)
    trace = sum(A[a][b] * D[b][a] for a in range(3) for b in range(3))
    shift = dlog - 0.5 * trace
    w = [A[a][0] * du[0] + A[a][1] * du[1] + A[a][2] * du[2] for a in range(3)]
    AD = [[A[a][0] * D[0][c] + A[a][1] * D[1][c] + A[a][2] * D[2][c] for c in range(3)] for a in range(3)]
    curve = [AD[a][0] * A[0][b] + AD[a][1] * A[1][b] + AD[a][2] * A[2][b] for a, b in DUOS]
    B = full(curve)
    au = [A[a][0] * u[0] + A[a][1] * u[1] + A[a][2] * u[2] for a in range(3)]
    bu = [B[a][0] * u[0] + B[a][1] * u[1] + B[a][2] * u[2] for a in range(3)]
    e0 = log_pre - 0.5 * (u[0] * au[0] + u[1] * au[1] + u[2] * au[2])
    expo = [e0] + au + [-0.5 * inv[n] if n < 3 else -inv[n] for n in range(6)]
    q0 = shift - (u[0] * w[0] + u[1] * w[1] + u[2] * w[2]) + 0.5 * (u[0] * bu[0] + u[1] * bu[1] + u[2] * bu[2])
    fact = [q0] + [w[a] - bu[a] for a in range(3)] + [0.5 * curve[n] if n < 3 else curve[n] for n in range(6)]
    return [x * LOG2E for x in expo], [x * -0.5 for x in fact]


def split3(x):
    hi = x.astype(BF16).astype(F32)
    r = x - hi
    mid = r.astype(BF16).astype(F32)
    return hi, mid, r - mid


def mirror(x, low_pair):
    return jnp.where(low_pair, pltpu.roll(x, 6, 0), pltpu.roll(x, 2, 0))


def kernel(
    state_hbm, tan_hbm, orient_hbm, walls_hbm, out_hbm,
    xs, xt, ob, tb, orient_v, bits, walls_v, mg, ml, vxy, xsp, part, rx1, sumt, tot,
    vsend, vrecv, xsend, xleft, xright, cs, csb, eq,
    lsem, s1, r1, s2, r2, ysem, xsem_s, xsem_r, osem,
):
    me = lax.axis_index("vert")
    gx = lax.axis_index("gx")
    gy = lax.axis_index("gy")
    wall = gy
    inner = 1 - gy
    load_t = pltpu.make_async_copy(tan_hbm, xt.at[pl.ds(0, ROWS)], lsem.at[0])
    load_s = pltpu.make_async_copy(state_hbm, xs.at[pl.ds(0, ROWS)], lsem.at[1])
    load_o = pltpu.make_async_copy(orient_hbm, orient_v, lsem.at[2])
    load_w = pltpu.make_async_copy(walls_hbm, walls_v, lsem.at[3])
    load_o.start()
    load_t.start()
    load_s.start()
    load_w.start()

    barrier = pltpu.get_barrier_semaphore()
    for d in ORDER:
        pl.semaphore_signal(barrier, inc=1, device_id={"vert": lax.rem(me + d, PEERS)}, device_id_type=MESH)
    pl.semaphore_signal(barrier, inc=1, device_id={"gy": inner}, device_id_type=MESH)
    east = lax.rem(gx + 1, 8)
    west = lax.rem(gx + 7, 8)
    pl.semaphore_signal(barrier, inc=1, device_id={"gx": east}, device_id_type=MESH)
    pl.semaphore_signal(barrier, inc=1, device_id={"gx": west}, device_id_type=MESH)

    zeros_tail = jnp.zeros((PAD_ROWS - ROWS, 128), F32)
    xs[pl.ds(ROWS, PAD_ROWS - ROWS), :] = zeros_tail
    xt[pl.ds(ROWS, PAD_ROWS - ROWS), :] = zeros_tail
    bits[...] = jnp.zeros((2, PAD), F32)
    load_o.wait()
    bits[:, 0:SLOTS] = orient_v[...].astype(F32)
    row = lax.broadcasted_iota(jnp.int32, (8, PAD), 0)
    slot = (lax.broadcasted_iota(jnp.int32, (8, PAD), 1) + me * SLOTS).astype(F32) + 0.5
    by40 = jnp.floor(slot * (1.0 / 40.0))
    by400 = jnp.floor(slot * (1.0 / 400.0))
    by4 = jnp.floor(slot * 0.25)
    sx = jnp.broadcast_to(bits[0:1, :], (8, PAD)) * 2.0 - 1.0
    sy = jnp.broadcast_to(bits[1:2, :], (8, PAD)) * 2.0 - 1.0
    vx = sx * (by40 - 10.0 * by400 + 0.5) * 0.5
    vy = sy * (by4 - 10.0 * by40 + 0.5) * 0.5
    vz = (by400 - 9.5) * 0.5
    quad = [vx * vx, vy * vy, vz * vz, vx * vy, vx * vz, vy * vz]
    qhi = [q.astype(BF16).astype(F32) for q in quad]
    qlo = [q - h for q, h in zip(quad, qhi)]
    lin = [jnp.ones((8, PAD), F32), vx, vy, vz]
    zero = jnp.zeros((8, PAD), F32)

    def pick(values):
        out = values[0]
        for k in range(1, 8):
            out = jnp.where(row == k, values[k], out)
        return out

    head = pick(lin + qhi[:4])
    tail = pick(qhi[4:] + qlo)
    lows = pick([zero] * 4 + qlo[:4])
    even = lax.rem(row, 2) == 0
    pair_hi = jnp.where(even, qhi[4], qhi[5])
    pair_lo = jnp.where(even, qlo[4], qlo[5])
    ml[...] = (jnp.concatenate([head, lows, pair_hi, pair_lo], axis=0) * 0.125).astype(BF16)
    table = jnp.concatenate([head, tail] * 3 + [zero] * 10, axis=0)
    mg[...] = jnp.transpose(table).astype(BF16)
    krow = lax.broadcasted_iota(jnp.int32, (128, 256), 0)
    kcol = lax.broadcasted_iota(jnp.int32, (128, 256), 1)
    choose = jnp.where(krow == 1 + (kcol >> 7), 1.0, 0.0).astype(BF16)
    vxy[...] = jnp.dot(mg[...], choose, preferred_element_type=F32)
    csb[...] = jnp.zeros(csb.shape, BF16)

    sub = lax.broadcasted_iota(jnp.int32, (8, 128), 0)
    lane = lax.broadcasted_iota(jnp.int32, (8, 128), 1)
    low_pair = lax.rem(sub, 4) < 2
    toward = (1 - 2 * gy).astype(F32)

    def comp(tile, coef, y):
        return xt[pl.ds(tile * 48 + coef * 2 + y, 8, stride=6), :]

    def speed_x(tile):
        return vxy[pl.ds(pl.multiple_of(tile * 8, 8), 8), 0:128]

    def speed_y(tile):
        return vxy[pl.ds(pl.multiple_of(tile * 8, 8), 8), 128:256]

    load_t.wait()

    def pack_rows(t, carry):
        traces = []
        for tile in (t, t + HALF):
            v = speed_y(tile)
            sgn = jnp.where(v > 0.0, 1.0, -1.0)
            value = comp(tile, 0, inner) + sgn * comp(tile, 2, inner)
            traces.append((v * toward > 0.0, value, comp(tile, 1, inner)))
        (in0, val0, slo0), (in1, val1, slo1) = traces
        base = pl.multiple_of(t * 16, 16)
        vsend[pl.ds(base, 8), :] = jnp.where(in0, val0, jnp.where(in1, val1, mirror(val1, low_pair)))
        vsend[pl.ds(base + 8, 8), :] = jnp.where(in0, slo0, jnp.where(in1, slo1, mirror(slo1, low_pair)))
        return carry

    lax.fori_loop(0, HALF, pack_rows, 0, unroll=2)
    pl.semaphore_wait(barrier, PEERS + 2)
    send_y = pltpu.make_async_remote_copy(
        src_ref=vsend, dst_ref=vrecv, send_sem=ysem.at[0], recv_sem=ysem.at[1],
        device_id={"gy": inner}, device_id_type=MESH,
    )
    send_y.start()

    def spread(ref, first):
        def body(t, carry):
            for j in range(6):
                hi, mid, lo = split3(ref[pl.ds(t * 96 + j, 16, stride=6), :])
                rows16 = pl.ds(pl.multiple_of(t * 16, 16), 16)
                cols = pl.ds((j % 2) * 128, 128)
                xsp[first + j // 2, 0, rows16, cols] = hi.astype(BF16)
                xsp[first + j // 2, 1, rows16, cols] = mid.astype(BF16)
                xsp[first + j // 2, 2, rows16, cols] = lo.astype(BF16)
            return carry

        lax.fori_loop(0, PAD // 16, body, 0)

    spread(xt, 3)
    load_s.wait()
    spread(xs, 0)
    group = sub // 2
    packed = [None] * 3
    for p in range(6):
        acc = jnp.dot(ml[...], xsp[p, 0], preferred_element_type=F32)
        acc += jnp.dot(ml[...], xsp[p, 1], preferred_element_type=F32)
        acc += jnp.dot(ml[...], xsp[p, 2], preferred_element_type=F32)
        for h in range(2):
            c = 2 * p + h
            cols = slice(h * 128, h * 128 + 128)
            part[pl.ds(c * 8, 8), :] = acc[0:8, cols] + acc[8:16, cols]
            extra = acc[16:24, cols] + acc[24:32, cols]
            old = packed[c // 4]
            packed[c // 4] = extra if old is None else jnp.where(group == c % 4, extra, old)
    for i in range(3):
        part[pl.ds((12 + i) * 8, 8), :] = packed[i]
    part[pl.ds(120, 8), :] = jnp.zeros((8, 128), F32)

    first = []
    for d in ORDER:
        peer = lax.rem(me + d, PEERS)
        copy = pltpu.make_async_remote_copy(
            src_ref=part.at[pl.ds(pl.multiple_of(peer * 8, 8), 8)],
            dst_ref=rx1.at[pl.ds((15 - d) * 8, 8)],
            send_sem=s1.at[d - 1], recv_sem=r1.at[d - 1],
            device_id={"vert": peer}, device_id_type=MESH,
        )
        copy.start()
        first.append(copy)

    def pack_cols(t, carry):
        acc0, acc1, signs = carry
        v = speed_x(t)
        right = v > 0.0
        sgn = jnp.where(right, 1.0, -1.0)
        for y in range(2):
            value = comp(t, 0, y) + sgn * comp(t, 1, y)
            slope = comp(t, 2, y)
            at = y * 64 + t
            here = lane == at
            edge0 = jnp.where(right, pltpu.roll(value, 1, 1), value)
            edge1 = jnp.where(right, pltpu.roll(slope, 1, 1), slope)
            acc0 = jnp.where(here, pltpu.roll(edge0, at, 1), acc0)
            acc1 = jnp.where(here, pltpu.roll(edge1, at, 1), acc1)
            signs = jnp.where(here, sgn, signs)
        return acc0, acc1, signs

    blank = jnp.zeros((8, 128), F32)
    acc0, acc1, signs = lax.fori_loop(0, TILES, pack_cols, (blank, blank, blank))
    xsend[0:8, :] = acc0
    xsend[8:16, :] = acc1
    send_e = pltpu.make_async_remote_copy(
        src_ref=xsend, dst_ref=xleft, send_sem=xsem_s.at[0], recv_sem=xsem_r.at[0],
        device_id={"gx": east}, device_id_type=MESH,
    )
    send_w = pltpu.make_async_remote_copy(
        src_ref=xsend, dst_ref=xright, send_sem=xsem_s.at[1], recv_sem=xsem_r.at[1],
        device_id={"gx": west}, device_id_type=MESH,
    )
    send_e.start()
    send_w.start()

    for copy in first:
        copy.wait_recv()
    mine = pl.ds(pl.multiple_of(me * 8, 8), 8)
    total = part[mine, :]
    for k in range(15):
        total = total + rx1[pl.ds(k * 8, 8), :]
    sumt[...] = total
    tot[mine, :] = total
    second = []
    for d in ORDER:
        copy = pltpu.make_async_remote_copy(
            src_ref=sumt, dst_ref=tot.at[mine],
            send_sem=s2.at[d - 1], recv_sem=r2.at[d - 1],
            device_id={"vert": lax.rem(me + d, PEERS)}, device_id_type=MESH,
        )
        copy.start()
        second.append(copy)

    send_e.wait_recv()
    send_w.wait_recv()
    from_left = signs > 0.0
    edge_val = jnp.where(from_left, xleft[0:8, :], xright[0:8, :])
    edge_slo = jnp.where(from_left, xleft[8:16, :], xright[8:16, :])
    send_y.wait_recv()
    load_w.wait()
    flags = walls_v[pl.ds(wall, 1), :].astype(F32)
    flag = jnp.broadcast_to(flags, (8, 128))

    def move(t, carry):
        base = pl.multiple_of(t * 16, 16)
        far = [vrecv[pl.ds(base, 8), :], vrecv[pl.ds(base + 8, 8), :]]
        first_in = None
        for n, tile in enumerate((t, t + HALF)):
            v_x = speed_x(tile)
            v_y = speed_y(tile)
            right = v_x > 0.0
            s_x = jnp.where(right, 1.0, -1.0)
            s_y = jnp.where(v_y > 0.0, 1.0, -1.0)
            a_x = jnp.abs(v_x)
            a_y = jnp.abs(v_y)
            inward = v_y * toward > 0.0
            if n == 0:
                first_in = inward
                halo = far
            else:
                halo = [jnp.where(first_in, f, mirror(f, low_pair)) for f in far]
            cw, gxw, gyw = (comp(tile, k, wall) for k in range(3))
            ci, gxi, gyi = (comp(tile, k, inner) for k in range(3))
            fw = cw + s_y * gyw
            fi = ci + s_y * gyi
            u_w = (
                jnp.where(inward, flag * mirror(fw, low_pair), fi),
                jnp.where(inward, flag * mirror(gxw, low_pair), gxi),
            )
            u_i = (jnp.where(inward, fw, halo[0]), jnp.where(inward, gxw, halo[1]))
            outermost = lane == jnp.where(right, 0, 127)
            for y, c, g_x, g_y, f_y, (uy0, uy1) in (
                (wall, cw, gxw, gyw, fw, u_w),
                (inner, ci, gxi, gyi, fi, u_i),
            ):
                f_x = c + s_x * g_x
                back = lax.rem(256 - (y * 64 + tile), 128)
                e0 = pltpu.roll(edge_val, back, 1)
                e1 = pltpu.roll(edge_slo, back, 1)
                e0 = jnp.where(right, e0, pltpu.roll(e0, 127, 1))
                e1 = jnp.where(right, e1, pltpu.roll(e1, 127, 1))
                ux0 = jnp.where(right, pltpu.roll(f_x, 1, 1), pltpu.roll(f_x, 127, 1))
                ux2 = jnp.where(right, pltpu.roll(g_y, 1, 1), pltpu.roll(g_y, 127, 1))
                ux0 = jnp.where(outermost, e0, ux0)
                ux2 = jnp.where(outermost, e1, ux2)
                c2 = c + c
                mean = a_x * (f_x - ux0) + a_y * (f_y - uy0) + c2
                rx = 3.0 * v_x * (f_x + ux0 - c2) + a_y * (g_x - uy1) + 2.0 * g_x
                ry = a_x * (g_y - ux2) + 3.0 * v_y * (f_y + uy0 - c2) + 2.0 * g_y
                for k, value in enumerate((mean, rx, ry)):
                    at = pl.multiple_of((tile * 6 + k * 2 + y) * 8, 8)
                    tb[pl.ds(at, 8), :] = value
        return carry

    lax.fori_loop(0, HALF, move, 0)

    for copy in second:
        copy.wait_recv()
    upper = sub >= 4
    q_of = lax.rem(sub, 4)
    xi = jnp.where(q_of >= 2, GAUSS, -GAUSS)
    eta = jnp.where(lax.rem(q_of, 2) == 1, GAUSS, -GAUSS)

    def moment(k):
        s, n = divmod(k, 10)
        coefs = []
        for j in range(6):
            c = s * 6 + j
            at = c * 8 + n if n < 8 else (12 + c // 4) * 8 + (c % 4) * 2 + n - 8
            coefs.append(jnp.broadcast_to(tot[pl.ds(at, 1), :], (8, 128)))
        a, b, c = (jnp.where(upper, coefs[2 * m + 1], coefs[2 * m]) for m in range(3))
        return a + xi * b + eta * c

    expo, fact = gauss_coefs([moment(k) for k in range(20)])
    for half, coefs in enumerate((expo, fact)):
        for k, x in enumerate(coefs):
            for n, piece in enumerate(split3(x)):
                for r in (k,) if k < 4 else (k, k + 6):
                    cs[pl.ds(half * 384 + n * 16 + r, 8, stride=48), :] = piece
    for i in range(8):
        csb[i, 0:48, 0:128] = cs[i * 48 : i * 48 + 48, :].astype(BF16)
        csb[i, 0:48, 128:256] = cs[384 + i * 48 : 384 + i * 48 + 48, :].astype(BF16)
    for i in range(8):
        eq[i] = jnp.dot(mg[...], csb[i], preferred_element_type=F32)

    stores = []
    quarter = TILES // 4
    for part_no in range(4):
        def finish(t, carry):
            rows8 = pl.ds(pl.multiple_of(t * 8, 8), 8)
            for y in range(2):
                g = [jnp.exp2(eq[y * 4 + q, rows8, 0:128]) * eq[y * 4 + q, rows8, 128:256] for q in range(4)]
                low = g[0] + g[1]
                high = g[2] + g[3]
                vals = (
                    low + high,
                    (3.0 * GAUSS) * (high - low),
                    (3.0 * GAUSS) * ((g[1] - g[0]) + (g[3] - g[2])),
                )
                for k in range(3):
                    at = pl.multiple_of((t * 6 + k * 2 + y) * 8, 8)
                    ob[pl.ds(t * 48 + k * 2 + y, 8, stride=6), :] = tb[pl.ds(at, 8), :] + vals[k]
            return carry

        lax.fori_loop(part_no * quarter, (part_no + 1) * quarter, finish, 0, unroll=2)
        begin = part_no * quarter * 48
        size = min(quarter * 48, ROWS - begin)
        store = pltpu.make_async_copy(ob.at[pl.ds(begin, size)], out_hbm.at[pl.ds(begin, size)], osem.at[part_no])
        store.start()
        stores.append(store)

    for copy in first + second + [send_y, send_e, send_w]:
        copy.wait_send()
    for store in stores:
        store.wait()


def shards(state, tangent, orient, walls):
    hbm = pl.BlockSpec(memory_space=pltpu.HBM)
    out = pl.pallas_call(
        kernel,
        out_shape=jax.ShapeDtypeStruct((ROWS, 128), F32),
        in_specs=[hbm] * 4,
        out_specs=hbm,
        scratch_shapes=[
            pltpu.VMEM((PAD_ROWS, 128), F32),
            pltpu.VMEM((PAD_ROWS, 128), F32),
            pltpu.VMEM((PAD_ROWS, 128), F32),
            pltpu.VMEM((PAD_ROWS, 128), F32),
            pltpu.VMEM((2, SLOTS), jnp.int32),
            pltpu.VMEM((2, PAD), F32),
            pltpu.VMEM((2, 128), jnp.int32),
            pltpu.VMEM((PAD, 128), BF16),
            pltpu.VMEM((32, PAD), BF16),
            pltpu.VMEM((PAD, 256), F32),
            pltpu.VMEM((6, 3, PAD, 256), BF16),
            pltpu.VMEM((128, 128), F32),
            pltpu.VMEM((120, 128), F32),
            pltpu.VMEM((8, 128), F32),
            pltpu.VMEM((128, 128), F32),
            pltpu.VMEM((HALF * 16, 128), F32),
            pltpu.VMEM((HALF * 16, 128), F32),
            pltpu.VMEM((16, 128), F32),
            pltpu.VMEM((16, 128), F32),
            pltpu.VMEM((16, 128), F32),
            pltpu.VMEM((16 * 48, 128), F32),
            pltpu.VMEM((8, 128, 256), BF16),
            pltpu.VMEM((8, PAD, 256), F32),
            pltpu.SemaphoreType.DMA((4,)),
            pltpu.SemaphoreType.DMA((15,)),
            pltpu.SemaphoreType.DMA((15,)),
            pltpu.SemaphoreType.DMA((15,)),
            pltpu.SemaphoreType.DMA((15,)),
            pltpu.SemaphoreType.DMA((2,)),
            pltpu.SemaphoreType.DMA((2,)),
            pltpu.SemaphoreType.DMA((2,)),
            pltpu.SemaphoreType.DMA((4,)),
        ],
        compiler_params=pltpu.CompilerParams(
            collective_id=0, has_side_effects=True, vmem_limit_bytes=60 * 1024 * 1024
        ),
    )(
        state.reshape(ROWS, 128),
        tangent.reshape(ROWS, 128),
        orient.T,
        walls,
    )
    return out.reshape(SLOTS, 3, 2, 128)


def solution(mesh):
    placed = (
        P("vert", None, "gy", "gx"),
        P("vert", None, "gy", "gx"),
        P("vert", None),
        P(None, "gx"),
    )
    return jax.shard_map(
        shards, mesh=mesh, in_specs=placed, out_specs=P("vert", None, "gy", "gx"), check_vma=False
    )
```

time: 194 us -> 36.1 us (0.19)
  waiting for transfers between devices: 79.8 us -> 0 us
  other arithmetic: 56.9 us -> 0 us
  Pallas kernels: 0 us -> 32.9 us
  local copies, waits for them, and re-layouts: 25 us -> 3.05 us
  between operations: 13.8 us -> 0.01 us
  starting transfers between devices: 13.2 us -> 0 us
  matrix products: 4.37 us -> 0 us
    psum x1 -> x0, waiting for transfers between devices: 77 us -> none  [shards(): params = gauss_params(lax.psum(partial_sums, 'vert'))]
    pallas_call x0 -> x1, Pallas kernels: none -> 32.9 us  [shards(): pl.pallas_call(kernel, out_shape=jax.ShapeDtypeStruct((ROWS, 128), F32),...]
    add x9 -> x0, other arithmetic: 21.2 us -> none  [the longest x1 6.21 us: transport(): speed_x * (right_val - left_val) + speed_y * (top_val - bottom_val)]
    mul x10 -> x0, other arithmetic: 18.3 us -> none  [the longest x1 16.4 us: gauss_tangent(): gauss * (params[10] + rel_x * params[11] + rel_y * params[12] + rel_z * p...]
    ppermute x4 -> x0, starting transfers between devices: 13.2 us -> none  [the longest x2 7.33 us: padded(): lax.ppermute(lax.slice_in_dim(block, block.shape[dim] - width, None, axis...]
    reshape x2 -> x0, local copies, waits for them, and re-layouts: 7.75 us -> none  [the longest x1 3.88 us: shards(): gauss_points(state).reshape(slots_here, point_count)]
    slice x3 -> x0, local copies, waits for them, and re-layouts: 6.1 us -> none  [the longest x2 6.09 us: padded(): lax.slice_in_dim(block, 0, width, axis=dim)]
    dot_general x1 -> x0, matrix products: 4.37 us -> none  [shards(): jnp.dot(moment_rows, stacked, precision=lax.Precision.HIGHEST, preferred_...]
  transfers between devices with their start and end apart: 5 -> 0, of which waited for: 3 -> 0; matrix products, arithmetic and copies ran while one was open for 20% -> 0% of each run, Pallas kernels for 0% -> 0%
where the time goes in v1:
time: 36.1 us; the launch traced here: 36 us
  Pallas kernels  32.9 us (91%)
  local copies, waits for them, and re-layouts  3.05 us (8%)
    pallas_call x1, Pallas kernels, shards(): pl.pallas_call(kernel, out_shape=jax.ShapeDtypeStruct((ROWS, 128), F32),...  32.9 us
    unnamed x1, local copies, waits for them, and re-layouts  3.05 us

profile of v1, /device:TPU:1, one launch (start us, length us, event | category | flops | bytes accessed | tf_op | source)
XLA Modules:
  0.0 36.0 jit_solution(939174037262772006)
XLA Ops:
  0.0 32.9 %shard_map.46 = f32[3000,128]{1,0:T(8,128)} custom-call(f32[3000,128]{1,0:T(8,128)} %bitcast.5, f32[3000,128]{1,0:T(8,128)} %bitcast.6, s32[2,500]{1,0:T(2,128)} %bitcast.7, s32[2,128]{1,0:T(2,128)} %walls_hbm.1), custom_call_target="tpu_custom_call" | custom-call | tf_op jit(solution)/shard_map/pallas_call | solution.py:425
  32.9 3.1 %copy.6 = f32[500,3,2,128]{3,2,1,0:T(2,128)} copy(f32[500,3,2,128]{3,2,1,0:T(2,128)} %bitcast.4) | data formatting | bytes 3072000

commit v2 on v1

--- a/solution.py
+++ b/solution.py
@@ -92,11 +92,11 @@
     return jnp.where(low_pair, pltpu.roll(x, 6, 0), pltpu.roll(x, 2, 0))
 
 
-def kernel(
-    state_hbm, tan_hbm, orient_hbm, walls_hbm, out_hbm,
-    xs, xt, ob, tb, orient_v, bits, walls_v, mg, ml, vxy, xsp, part, rx1, sumt, tot,
-    vsend, vrecv, xsend, xleft, xright, cs, csb, eq,
-    lsem, s1, r1, s2, r2, ysem, xsem_s, xsem_r, osem,
+def gather(
+    state_hbm, tan_hbm, orient_hbm, walls_hbm, tb, mg, csb,
+    xs, xt, orient_v, bits, walls_v, ml, vxy, xsp, part, rx1, sumt, tot,
+    vsend, vrecv, xsend, xleft, xright, edges, cs,
+    lsem, s1, r1, s2, r2, ysem, xsem_s, xsem_r,
 ):
     me = lax.axis_index("vert")
     gx = lax.axis_index("gx")
@@ -193,13 +193,7 @@
         vsend[pl.ds(base + 8, 8), :] = jnp.where(in0, slo0, jnp.where(in1, slo1, mirror(slo1, low_pair)))
         return carry
 
-    lax.fori_loop(0, HALF, pack_rows, 0, unroll=2)
-    pl.semaphore_wait(barrier, PEERS + 2)
-    send_y = pltpu.make_async_remote_copy(
-        src_ref=vsend, dst_ref=vrecv, send_sem=ysem.at[0], recv_sem=ysem.at[1],
-        device_id={"gy": inner}, device_id_type=MESH,
-    )
-    send_y.start()
+    lax.fori_loop(0, HALF, pack_rows, 0, unroll=4)
 
     def spread(ref, first):
         def body(t, carry):
@@ -215,6 +209,12 @@
         lax.fori_loop(0, PAD // 16, body, 0)
 
     spread(xt, 3)
+    pl.semaphore_wait(barrier, PEERS + 2)
+    send_y = pltpu.make_async_remote_copy(
+        src_ref=vsend, dst_ref=vrecv, send_sem=ysem.at[0], recv_sem=ysem.at[1],
+        device_id={"gy": inner}, device_id_type=MESH,
+    )
+    send_y.start()
     load_s.wait()
     spread(xs, 0)
     group = sub // 2
@@ -246,27 +246,22 @@
         copy.start()
         first.append(copy)
 
-    def pack_cols(t, carry):
-        acc0, acc1, signs = carry
-        v = speed_x(t)
-        right = v > 0.0
-        sgn = jnp.where(right, 1.0, -1.0)
-        for y in range(2):
-            value = comp(t, 0, y) + sgn * comp(t, 1, y)
-            slope = comp(t, 2, y)
-            at = y * 64 + t
-            here = lane == at
-            edge0 = jnp.where(right, pltpu.roll(value, 1, 1), value)
-            edge1 = jnp.where(right, pltpu.roll(slope, 1, 1), slope)
-            acc0 = jnp.where(here, pltpu.roll(edge0, at, 1), acc0)
-            acc1 = jnp.where(here, pltpu.roll(edge1, at, 1), acc1)
-            signs = jnp.where(here, sgn, signs)
-        return acc0, acc1, signs
-
-    blank = jnp.zeros((8, 128), F32)
-    acc0, acc1, signs = lax.fori_loop(0, TILES, pack_cols, (blank, blank, blank))
-    xsend[0:8, :] = acc0
-    xsend[8:16, :] = acc1
+    def pack_cols(v, carry):
+        acc = jnp.zeros((8, 128), F32)
+        for n in range(HALF):
+            tile = v * HALF + n
+            right = speed_x(tile) > 0.0
+            sgn = jnp.where(right, 1.0, -1.0)
+            for y in range(2):
+                value = comp(tile, 0, y) + sgn * comp(tile, 1, y)
+                for k, x in enumerate((value, comp(tile, 2, y))):
+                    at = n * 4 + y * 2 + k
+                    moved = jnp.where(right, pltpu.roll(x, (at + 1) % 128, 1), pltpu.roll(x, at, 1) if at else x)
+                    acc = jnp.where(lane == at, moved, acc)
+        xsend[pl.ds(pl.multiple_of(v * 8, 8), 8), :] = acc
+        return carry
+
+    lax.fori_loop(0, 2, pack_cols, 0)
     send_e = pltpu.make_async_remote_copy(
         src_ref=xsend, dst_ref=xleft, send_sem=xsem_s.at[0], recv_sem=xsem_r.at[0],
         device_id={"gx": east}, device_id_type=MESH,
@@ -298,9 +293,21 @@
 
     send_e.wait_recv()
     send_w.wait_recv()
-    from_left = signs > 0.0
-    edge_val = jnp.where(from_left, xleft[0:8, :], xright[0:8, :])
-    edge_slo = jnp.where(from_left, xleft[8:16, :], xright[8:16, :])
+
+    def unpack_cols(v, carry):
+        rows8 = pl.ds(pl.multiple_of(v * 8, 8), 8)
+        west_in = xleft[rows8, :]
+        east_in = xright[rows8, :]
+        for n in range(HALF):
+            tile = v * HALF + n
+            right = speed_x(tile) > 0.0
+            for k in range(4):
+                at = slice(n * 4 + k, n * 4 + k + 1)
+                value = jnp.where(right, jnp.broadcast_to(west_in[:, at], (8, 128)), jnp.broadcast_to(east_in[:, at], (8, 128)))
+                edges[pl.ds(pl.multiple_of((tile * 4 + k) * 8, 8), 8), :] = value
+        return carry
+
+    lax.fori_loop(0, 2, unpack_cols, 0)
     send_y.wait_recv()
     load_w.wait()
     flags = walls_v[pl.ds(wall, 1), :].astype(F32)
@@ -339,11 +346,9 @@
                 (inner, ci, gxi, gyi, fi, u_i),
             ):
                 f_x = c + s_x * g_x
-                back = lax.rem(256 - (y * 64 + tile), 128)
-                e0 = pltpu.roll(edge_val, back, 1)
-                e1 = pltpu.roll(edge_slo, back, 1)
-                e0 = jnp.where(right, e0, pltpu.roll(e0, 127, 1))
-                e1 = jnp.where(right, e1, pltpu.roll(e1, 127, 1))
+                at = pl.multiple_of((tile * 4 + y * 2) * 8, 8)
+                e0 = edges[pl.ds(at, 8), :]
+                e1 = edges[pl.ds(at + 8, 8), :]
                 ux0 = jnp.where(right, pltpu.roll(f_x, 1, 1), pltpu.roll(f_x, 127, 1))
                 ux2 = jnp.where(right, pltpu.roll(g_y, 1, 1), pltpu.roll(g_y, 127, 1))
                 ux0 = jnp.where(outermost, e0, ux0)
@@ -357,7 +362,7 @@
                     tb[pl.ds(at, 8), :] = value
         return carry
 
-    lax.fori_loop(0, HALF, move, 0)
+    lax.fori_loop(0, HALF, move, 0, unroll=2)
 
     for copy in second:
         copy.wait_recv()
@@ -385,6 +390,11 @@
     for i in range(8):
         csb[i, 0:48, 0:128] = cs[i * 48 : i * 48 + 48, :].astype(BF16)
         csb[i, 0:48, 128:256] = cs[384 + i * 48 : 384 + i * 48 + 48, :].astype(BF16)
+    for copy in first + second + [send_y, send_e, send_w]:
+        copy.wait_send()
+
+
+def collide(tb, mg, csb, out_hbm, eq, ob, osem):
     for i in range(8):
         eq[i] = jnp.dot(mg[...], csb[i], preferred_element_type=F32)
 
@@ -407,35 +417,34 @@
                     ob[pl.ds(t * 48 + k * 2 + y, 8, stride=6), :] = tb[pl.ds(at, 8), :] + vals[k]
             return carry
 
-        lax.fori_loop(part_no * quarter, (part_no + 1) * quarter, finish, 0, unroll=2)
+        lax.fori_loop(part_no * quarter, (part_no + 1) * quarter, finish, 0, unroll=4)
         begin = part_no * quarter * 48
         size = min(quarter * 48, ROWS - begin)
         store = pltpu.make_async_copy(ob.at[pl.ds(begin, size)], out_hbm.at[pl.ds(begin, size)], osem.at[part_no])
         store.start()
         stores.append(store)
-
-    for copy in first + second + [send_y, send_e, send_w]:
-        copy.wait_send()
     for store in stores:
         store.wait()
 
 
 def shards(state, tangent, orient, walls):
     hbm = pl.BlockSpec(memory_space=pltpu.HBM)
-    out = pl.pallas_call(
-        kernel,
-        out_shape=jax.ShapeDtypeStruct((ROWS, 128), F32),
+    vmem = pl.BlockSpec(memory_space=pltpu.VMEM)
+    tb, mg, csb = pl.pallas_call(
+        gather,
+        out_shape=(
+            pltpu.VMEM((PAD_ROWS, 128), F32),
+            pltpu.VMEM((PAD, 128), BF16),
+            pltpu.VMEM((8, 128, 256), BF16),
+        ),
         in_specs=[hbm] * 4,
-        out_specs=hbm,
+        out_specs=[vmem] * 3,
         scratch_shapes=[
-            pltpu.VMEM((PAD_ROWS, 128), F32),
-            pltpu.VMEM((PAD_ROWS, 128), F32),
             pltpu.VMEM((PAD_ROWS, 128), F32),
             pltpu.VMEM((PAD_ROWS, 128), F32),
             pltpu.VMEM((2, SLOTS), jnp.int32),
             pltpu.VMEM((2, PAD), F32),
             pltpu.VMEM((2, 128), jnp.int32),
-            pltpu.VMEM((PAD, 128), BF16),
             pltpu.VMEM((32, PAD), BF16),
             pltpu.VMEM((PAD, 256), F32),
             pltpu.VMEM((6, 3, PAD, 256), BF16),
@@ -448,9 +457,8 @@
             pltpu.VMEM((16, 128), F32),
             pltpu.VMEM((16, 128), F32),
             pltpu.VMEM((16, 128), F32),
+            pltpu.VMEM((TILES * 32, 128), F32),
             pltpu.VMEM((16 * 48, 128), F32),
-            pltpu.VMEM((8, 128, 256), BF16),
-            pltpu.VMEM((8, PAD, 256), F32),
             pltpu.SemaphoreType.DMA((4,)),
             pltpu.SemaphoreType.DMA((15,)),
             pltpu.SemaphoreType.DMA((15,)),
@@ -459,10 +467,9 @@
             pltpu.SemaphoreType.DMA((2,)),
             pltpu.SemaphoreType.DMA((2,)),
             pltpu.SemaphoreType.DMA((2,)),
-            pltpu.SemaphoreType.DMA((4,)),
         ],
         compiler_params=pltpu.CompilerParams(
-            collective_id=0, has_side_effects=True, vmem_limit_bytes=60 * 1024 * 1024
+            collective_id=0, has_side_effects=True, vmem_limit_bytes=58 * 1024 * 1024
         ),
     )(
         state.reshape(ROWS, 128),
@@ -470,6 +477,18 @@
         orient.T,
         walls,
     )
+    out = pl.pallas_call(
+        collide,
+        out_shape=jax.ShapeDtypeStruct((ROWS, 128), F32),
+        in_specs=[vmem] * 3,
+        out_specs=hbm,
+        scratch_shapes=[
+            pltpu.VMEM((8, PAD, 256), F32),
+            pltpu.VMEM((PAD_ROWS, 128), F32),
+            pltpu.SemaphoreType.DMA((4,)),
+        ],
+        compiler_params=pltpu.CompilerParams(vmem_limit_bytes=16 * 1024 * 1024),
+    )(tb, mg, csb)
     return out.reshape(SLOTS, 3, 2, 128)
 
 

time: 36.1 us -> 24.3 us (0.67)
  Pallas kernels: 32.9 us -> 24.1 us
  local copies, waits for them, and re-layouts: 3.05 us -> 0 us
    pallas_call x1 -> x2, Pallas kernels: 32.9 us -> 24.1 us  [the longest x1 22.1 us: shards(): pl.pallas_call(gather, out_shape=(pltpu.VMEM((PAD_ROWS, 128), F32), pltpu...]
    unnamed x1 -> x0, local copies, waits for them, and re-layouts: 3.05 us -> none
where the time goes in v2:
time: 24.3 us; the launch traced here: 24.2 us
  Pallas kernels  24.1 us (99%)
    pallas_call x1, Pallas kernels, shards(): pl.pallas_call(gather, out_shape=(pltpu.VMEM((PAD_ROWS, 128), F32), pltpu...  22.1 us
    pallas_call x1, Pallas kernels, shards(): pl.pallas_call(collide, out_shape=jax.ShapeDtypeStruct((ROWS, 128), F32),...  2.08 us

profile of v2, /device:TPU:1, one launch (start us, length us, event | category | flops | bytes accessed | tf_op | source)
XLA Modules:
  0.0 24.2 jit_solution(8583763406394461341)
XLA Ops:
  0.0 22.1 %shard_map.46 = (f32[3072,128]{1,0:T(8,128)S(1)}, bf16[512,128]{1,0:T(8,128)(2,1)S(1)}, bf16[8,128,256]{2,1,0:T(8,128)(2,1)S(1)}) custom-call(f32[3000,128]{1,0:T(8,128)} %bitcast.4, f32[3000,128]{1,0:T(8,128)} %bitcast.5, s32[2,500]{1,0:T(2,128)} %bitcast.6, s32[2,128]{1,0:T(2,128)} %walls_hbm.1), custom_call_target="tpu_custom_call" | custom-call | tf_op jit(solution)/shard_map/pallas_call | solution.py:433
  22.1 2.1 %shard_map.47 = f32[3000,128]{1,0:T(8,128)} custom-call(f32[3072,128]{1,0:T(8,128)S(1)} %get-tuple-element.8.tb, bf16[512,128]{1,0:T(8,128)(2,1)S(1)} %get-tuple-element.9.mg, bf16[8,128,256]{2,1,0:T(8,128)(2,1)S(1)} %get-tuple-element.10.csb), custom_call_target="tpu_custom_call" | custom-call | tf_op jit(solution)/shard_map/pallas_call | solution.py:480

commit v3 on v2

--- a/solution.py
+++ b/solution.py
@@ -23,6 +23,7 @@
 LOG2E = math.log2(math.e)
 DUOS = ((0, 0), (1, 1), (2, 2), (0, 1), (0, 2), (1, 2))
 PEERS = 16
+PARTS = 4
 ORDER = (8, 7, 9, 6, 10, 5, 11, 4, 12, 3, 13, 2, 14, 1, 15)
 
 
@@ -95,7 +96,7 @@
 def gather(
     state_hbm, tan_hbm, orient_hbm, walls_hbm, tb, mg, csb,
     xs, xt, orient_v, bits, walls_v, ml, vxy, xsp, part, rx1, sumt, tot,
-    vsend, vrecv, xsend, xleft, xright, edges, cs,
+    vsend, relay, vrecv, xsend, xleft, xright, edges, cs,
     lsem, s1, r1, s2, r2, ysem, xsem_s, xsem_r,
 ):
     me = lax.axis_index("vert")
@@ -115,7 +116,11 @@
     barrier = pltpu.get_barrier_semaphore()
     for d in ORDER:
         pl.semaphore_signal(barrier, inc=1, device_id={"vert": lax.rem(me + d, PEERS)}, device_id_type=MESH)
-    pl.semaphore_signal(barrier, inc=1, device_id={"gy": inner}, device_id_type=MESH)
+    odd = lax.rem(gx, 2)
+    side = gx + 1 - 2 * odd
+    plus = {"gx": side, "gy": lax.rem(gy + odd, 2)}
+    minus = {"gx": side, "gy": lax.rem(gy + odd + 1, 2)}
+    pl.semaphore_signal(barrier, inc=1, device_id={"gx": side, "gy": inner}, device_id_type=MESH)
     east = lax.rem(gx + 1, 8)
     west = lax.rem(gx + 7, 8)
     pl.semaphore_signal(barrier, inc=1, device_id={"gx": east}, device_id_type=MESH)
@@ -210,11 +215,23 @@
 
     spread(xt, 3)
     pl.semaphore_wait(barrier, PEERS + 2)
-    send_y = pltpu.make_async_remote_copy(
-        src_ref=vsend, dst_ref=vrecv, send_sem=ysem.at[0], recv_sem=ysem.at[1],
-        device_id={"gy": inner}, device_id_type=MESH,
-    )
-    send_y.start()
+    halves = (pl.ds(0, HALF * 8), pl.ds(HALF * 8, HALF * 8))
+    hop1 = [
+        pltpu.make_async_remote_copy(
+            src_ref=vsend.at[halves[n]], dst_ref=relay.at[halves[n]], send_sem=ysem.at[0, n], recv_sem=ysem.at[1, n],
+            device_id=to, device_id_type=MESH,
+        )
+        for n, to in enumerate((plus, minus))
+    ]
+    hop2 = [
+        pltpu.make_async_remote_copy(
+            src_ref=relay.at[halves[n]], dst_ref=vrecv.at[halves[n]], send_sem=ysem.at[2, n], recv_sem=ysem.at[3, n],
+            device_id=to, device_id_type=MESH,
+        )
+        for n, to in enumerate((plus, minus))
+    ]
+    for copy in hop1:
+        copy.start()
     load_s.wait()
     spread(xs, 0)
     group = sub // 2
@@ -273,6 +290,10 @@
     send_e.start()
     send_w.start()
 
+    for came, goes in zip(hop1, hop2):
+        came.wait_recv()
+        goes.start()
+
     for copy in first:
         copy.wait_recv()
     mine = pl.ds(pl.multiple_of(me * 8, 8), 8)
@@ -308,16 +329,12 @@
         return carry
 
     lax.fori_loop(0, 2, unpack_cols, 0)
-    send_y.wait_recv()
     load_w.wait()
     flags = walls_v[pl.ds(wall, 1), :].astype(F32)
     flag = jnp.broadcast_to(flags, (8, 128))
 
     def move(t, carry):
-        base = pl.multiple_of(t * 16, 16)
-        far = [vrecv[pl.ds(base, 8), :], vrecv[pl.ds(base + 8, 8), :]]
-        first_in = None
-        for n, tile in enumerate((t, t + HALF)):
+        for tile in (t, t + HALF):
             v_x = speed_x(tile)
             v_y = speed_y(tile)
             right = v_x > 0.0
@@ -326,11 +343,6 @@
             a_x = jnp.abs(v_x)
             a_y = jnp.abs(v_y)
             inward = v_y * toward > 0.0
-            if n == 0:
-                first_in = inward
-                halo = far
-            else:
-                halo = [jnp.where(first_in, f, mirror(f, low_pair)) for f in far]
             cw, gxw, gyw = (comp(tile, k, wall) for k in range(3))
             ci, gxi, gyi = (comp(tile, k, inner) for k in range(3))
             fw = cw + s_y * gyw
@@ -339,7 +351,7 @@
                 jnp.where(inward, flag * mirror(fw, low_pair), fi),
                 jnp.where(inward, flag * mirror(gxw, low_pair), gxi),
             )
-            u_i = (jnp.where(inward, fw, halo[0]), jnp.where(inward, gxw, halo[1]))
+            u_i = (jnp.where(inward, fw, 0.0), jnp.where(inward, gxw, 0.0))
             outermost = lane == jnp.where(right, 0, 127)
             for y, c, g_x, g_y, f_y, (uy0, uy1) in (
                 (wall, cw, gxw, gyw, fw, u_w),
@@ -364,6 +376,25 @@
 
     lax.fori_loop(0, HALF, move, 0, unroll=2)
 
+    for copy in hop2:
+        copy.wait_recv()
+
+    def add_halo(t, carry):
+        base = pl.multiple_of(t * 16, 16)
+        near = [vrecv[pl.ds(base, 8), :], vrecv[pl.ds(base + 8, 8), :]]
+        first_in = speed_y(t) * toward > 0.0
+        for tile in (t, t + HALF):
+            v_y = speed_y(tile)
+            speed = jnp.where(v_y * toward > 0.0, 0.0, v_y)
+            value, slope = near if tile is t else [jnp.where(first_in, f, mirror(f, low_pair)) for f in near]
+            a_y = jnp.abs(speed)
+            for k, term in enumerate((-a_y * value, -a_y * slope, 3.0 * speed * value)):
+                at = pl.ds(pl.multiple_of((tile * 6 + k * 2 + inner) * 8, 8), 8)
+                tb[at, :] = tb[at, :] + term
+        return carry
+
+    lax.fori_loop(0, HALF, add_halo, 0, unroll=4)
+
     for copy in second:
         copy.wait_recv()
     upper = sub >= 4
@@ -390,19 +421,19 @@
     for i in range(8):
         csb[i, 0:48, 0:128] = cs[i * 48 : i * 48 + 48, :].astype(BF16)
         csb[i, 0:48, 128:256] = cs[384 + i * 48 : 384 + i * 48 + 48, :].astype(BF16)
-    for copy in first + second + [send_y, send_e, send_w]:
+    for copy in first + second + hop1 + hop2 + [send_e, send_w]:
         copy.wait_send()
 
 
 def collide(tb, mg, csb, out_hbm, eq, ob, osem):
-    for i in range(8):
-        eq[i] = jnp.dot(mg[...], csb[i], preferred_element_type=F32)
-
     stores = []
-    quarter = TILES // 4
-    for part_no in range(4):
-        def finish(t, carry):
-            rows8 = pl.ds(pl.multiple_of(t * 8, 8), 8)
+    tiles = TILES // PARTS
+    for n in range(PARTS):
+        rows = slice(n * tiles * 8, (n + 1) * tiles * 8)
+        for i in range(8):
+            eq[i, rows, :] = jnp.dot(mg[rows, :], csb[i], preferred_element_type=F32)
+        for t in range(n * tiles, (n + 1) * tiles):
+            rows8 = slice(t * 8, t * 8 + 8)
             for y in range(2):
                 g = [jnp.exp2(eq[y * 4 + q, rows8, 0:128]) * eq[y * 4 + q, rows8, 128:256] for q in range(4)]
                 low = g[0] + g[1]
@@ -413,14 +444,11 @@
                     (3.0 * GAUSS) * ((g[1] - g[0]) + (g[3] - g[2])),
                 )
                 for k in range(3):
-                    at = pl.multiple_of((t * 6 + k * 2 + y) * 8, 8)
-                    ob[pl.ds(t * 48 + k * 2 + y, 8, stride=6), :] = tb[pl.ds(at, 8), :] + vals[k]
-            return carry
-
-        lax.fori_loop(part_no * quarter, (part_no + 1) * quarter, finish, 0, unroll=4)
-        begin = part_no * quarter * 48
-        size = min(quarter * 48, ROWS - begin)
-        store = pltpu.make_async_copy(ob.at[pl.ds(begin, size)], out_hbm.at[pl.ds(begin, size)], osem.at[part_no])
+                    at = (t * 6 + k * 2 + y) * 8
+                    ob[pl.ds(t * 48 + k * 2 + y, 8, stride=6), :] = tb[at : at + 8, :] + vals[k]
+        begin = n * tiles * 48
+        size = min(tiles * 48, ROWS - begin)
+        store = pltpu.make_async_copy(ob.at[pl.ds(begin, size)], out_hbm.at[pl.ds(begin, size)], osem.at[n])
         store.start()
         stores.append(store)
     for store in stores:
@@ -454,6 +482,7 @@
             pltpu.VMEM((128, 128), F32),
             pltpu.VMEM((HALF * 16, 128), F32),
             pltpu.VMEM((HALF * 16, 128), F32),
+            pltpu.VMEM((HALF * 16, 128), F32),
             pltpu.VMEM((16, 128), F32),
             pltpu.VMEM((16, 128), F32),
             pltpu.VMEM((16, 128), F32),
@@ -464,7 +493,7 @@
             pltpu.SemaphoreType.DMA((15,)),
             pltpu.SemaphoreType.DMA((15,)),
             pltpu.SemaphoreType.DMA((15,)),
-            pltpu.SemaphoreType.DMA((2,)),
+            pltpu.SemaphoreType.DMA((4, 2)),
             pltpu.SemaphoreType.DMA((2,)),
             pltpu.SemaphoreType.DMA((2,)),
         ],
@@ -485,7 +514,7 @@
         scratch_shapes=[
             pltpu.VMEM((8, PAD, 256), F32),
             pltpu.VMEM((PAD_ROWS, 128), F32),
-            pltpu.SemaphoreType.DMA((4,)),
+            pltpu.SemaphoreType.DMA((PARTS,)),
         ],
         compiler_params=pltpu.CompilerParams(vmem_limit_bytes=16 * 1024 * 1024),
     )(tb, mg, csb)

time: 24.3 us -> 21.9 us (0.901)
  Pallas kernels: 24.1 us -> 21.8 us
    pallas_call x1, Pallas kernels: 22.1 us -> 20.4 us  [shards(): pl.pallas_call(gather, out_shape=(pltpu.VMEM((PAD_ROWS, 128), F32), pltpu...]
    pallas_call x1, Pallas kernels: 2.08 us -> 1.48 us  [shards(): pl.pallas_call(collide, out_shape=jax.ShapeDtypeStruct((ROWS, 128), F32),...]
where the time goes in v3:
time: 21.9 us; the launch traced here: 21.8 us
  Pallas kernels  21.8 us (100%)
    pallas_call x1, Pallas kernels, shards(): pl.pallas_call(gather, out_shape=(pltpu.VMEM((PAD_ROWS, 128), F32), pltpu...  20.4 us
    pallas_call x1, Pallas kernels, shards(): pl.pallas_call(collide, out_shape=jax.ShapeDtypeStruct((ROWS, 128), F32),...  1.48 us

profile of v3, /device:TPU:1, one launch (start us, length us, event | category | flops | bytes accessed | tf_op | source)
XLA Modules:
  0.0 21.8 jit_solution(4470094615623221468)
XLA Ops:
  0.0 20.4 %shard_map.46 = (f32[3072,128]{1,0:T(8,128)S(1)}, bf16[512,128]{1,0:T(8,128)(2,1)S(1)}, bf16[8,128,256]{2,1,0:T(8,128)(2,1)S(1)}) custom-call(f32[3000,128]{1,0:T(8,128)} %bitcast.4, f32[3000,128]{1,0:T(8,128)} %bitcast.5, s32[2,500]{1,0:T(2,128)} %bitcast.6, s32[2,128]{1,0:T(2,128)} %walls_hbm.1), custom_call_target="tpu_custom_call" | custom-call | tf_op jit(solution)/shard_map/pallas_call | solution.py:461
  20.4 1.5 %shard_map.47 = f32[3000,128]{1,0:T(8,128)} custom-call(f32[3072,128]{1,0:T(8,128)S(1)} %get-tuple-element.8.tb, bf16[512,128]{1,0:T(8,128)(2,1)S(1)} %get-tuple-element.9.mg, bf16[8,128,256]{2,1,0:T(8,128)(2,1)S(1)} %get-tuple-element.10.csb), custom_call_target="tpu_custom_call" | custom-call | tf_op jit(solution)/shard_map/pallas_call | solution.py:509

commit v4 on v3

--- a/solution.py
+++ b/solution.py
@@ -95,8 +95,8 @@
 
 def gather(
     state_hbm, tan_hbm, orient_hbm, walls_hbm, tb, mg, csb,
-    xs, xt, orient_v, bits, walls_v, ml, vxy, xsp, part, rx1, sumt, tot,
-    vsend, relay, vrecv, xsend, xleft, xright, edges, cs,
+    xs, xt, orient_v, bits, walls_v, ml, vxy, part, rx1, sumt, tot,
+    vsend, relay, vrecv, xsend, xside, xleft, xright, cs,
     lsem, s1, r1, s2, r2, ysem, xsem_s, xsem_r,
 ):
     me = lax.axis_index("vert")
@@ -200,21 +200,46 @@
 
     lax.fori_loop(0, HALF, pack_rows, 0, unroll=4)
 
-    def spread(ref, first):
-        def body(t, carry):
-            for j in range(6):
-                hi, mid, lo = split3(ref[pl.ds(t * 96 + j, 16, stride=6), :])
-                rows16 = pl.ds(pl.multiple_of(t * 16, 16), 16)
-                cols = pl.ds((j % 2) * 128, 128)
-                xsp[first + j // 2, 0, rows16, cols] = hi.astype(BF16)
-                xsp[first + j // 2, 1, rows16, cols] = mid.astype(BF16)
-                xsp[first + j // 2, 2, rows16, cols] = lo.astype(BF16)
-            return carry
-
-        lax.fori_loop(0, PAD // 16, body, 0)
-
-    spread(xt, 3)
+    group = sub // 2
+    packed = [None] * 3
+
+    def sums(ref, first):
+        for p in range(3):
+            acc = None
+            for k in range(2):
+                pair = [ref[pl.ds(k * 1536 + 2 * p + h, 256, stride=6), :] for h in range(2)]
+                for piece in split3(jnp.concatenate(pair, axis=1)):
+                    got = jnp.dot(ml[:, k * 256 : k * 256 + 256], piece.astype(BF16), preferred_element_type=F32)
+                    acc = got if acc is None else acc + got
+            for h in range(2):
+                c = first + 2 * p + h
+                cols = slice(h * 128, h * 128 + 128)
+                part[pl.ds(c * 8, 8), :] = acc[0:8, cols] + acc[8:16, cols]
+                extra = acc[16:24, cols] + acc[24:32, cols]
+                old = packed[c // 4]
+                packed[c // 4] = extra if old is None else jnp.where(group == c % 4, extra, old)
+
+    sums(xt, 6)
+    load_s.wait()
+    sums(xs, 0)
+    for i in range(3):
+        part[pl.ds((12 + i) * 8, 8), :] = packed[i]
+    part[pl.ds(120, 8), :] = jnp.zeros((8, 128), F32)
+
     pl.semaphore_wait(barrier, PEERS + 2)
+
+    first = []
+    for d in ORDER:
+        peer = lax.rem(me + d, PEERS)
+        copy = pltpu.make_async_remote_copy(
+            src_ref=part.at[pl.ds(pl.multiple_of(lax.rem(peer, 8) * 16, 16), 16)],
+            dst_ref=rx1.at[pl.ds((15 - d) * 16, 16)],
+            send_sem=s1.at[d - 1], recv_sem=r1.at[d - 1],
+            device_id={"vert": peer}, device_id_type=MESH,
+        )
+        copy.start()
+        first.append(copy)
+
     halves = (pl.ds(0, HALF * 8), pl.ds(HALF * 8, HALF * 8))
     hop1 = [
         pltpu.make_async_remote_copy(
@@ -232,42 +257,17 @@
     ]
     for copy in hop1:
         copy.start()
-    load_s.wait()
-    spread(xs, 0)
-    group = sub // 2
-    packed = [None] * 3
-    for p in range(6):
-        acc = jnp.dot(ml[...], xsp[p, 0], preferred_element_type=F32)
-        acc += jnp.dot(ml[...], xsp[p, 1], preferred_element_type=F32)
-        acc += jnp.dot(ml[...], xsp[p, 2], preferred_element_type=F32)
-        for h in range(2):
-            c = 2 * p + h
-            cols = slice(h * 128, h * 128 + 128)
-            part[pl.ds(c * 8, 8), :] = acc[0:8, cols] + acc[8:16, cols]
-            extra = acc[16:24, cols] + acc[24:32, cols]
-            old = packed[c // 4]
-            packed[c // 4] = extra if old is None else jnp.where(group == c % 4, extra, old)
-    for i in range(3):
-        part[pl.ds((12 + i) * 8, 8), :] = packed[i]
-    part[pl.ds(120, 8), :] = jnp.zeros((8, 128), F32)
-
-    first = []
-    for d in ORDER:
-        peer = lax.rem(me + d, PEERS)
-        copy = pltpu.make_async_remote_copy(
-            src_ref=part.at[pl.ds(pl.multiple_of(peer * 8, 8), 8)],
-            dst_ref=rx1.at[pl.ds((15 - d) * 8, 8)],
-            send_sem=s1.at[d - 1], recv_sem=r1.at[d - 1],
-            device_id={"vert": peer}, device_id_type=MESH,
-        )
-        copy.start()
-        first.append(copy)
+
+    quad_lane = lane >> 2
 
     def pack_cols(v, carry):
         acc = jnp.zeros((8, 128), F32)
+        sides = acc
         for n in range(HALF):
             tile = v * HALF + n
-            right = speed_x(tile) > 0.0
+            speed = speed_x(tile)
+            right = speed > 0.0
+            sides = jnp.where(quad_lane == n, speed, sides)
             sgn = jnp.where(right, 1.0, -1.0)
             for y in range(2):
                 value = comp(tile, 0, y) + sgn * comp(tile, 1, y)
@@ -276,6 +276,7 @@
                     moved = jnp.where(right, pltpu.roll(x, (at + 1) % 128, 1), pltpu.roll(x, at, 1) if at else x)
                     acc = jnp.where(lane == at, moved, acc)
         xsend[pl.ds(pl.multiple_of(v * 8, 8), 8), :] = acc
+        xside[pl.ds(pl.multiple_of(v * 8, 8), 8), :] = sides
         return carry
 
     lax.fori_loop(0, 2, pack_cols, 0)
@@ -296,39 +297,26 @@
 
     for copy in first:
         copy.wait_recv()
-    mine = pl.ds(pl.multiple_of(me * 8, 8), 8)
-    total = part[mine, :]
+    chunk = pl.ds(pl.multiple_of(lax.rem(me, 8) * 16, 16), 16)
+    total = part[chunk, :]
     for k in range(15):
-        total = total + rx1[pl.ds(k * 8, 8), :]
+        total = total + rx1[pl.ds(k * 16, 16), :]
     sumt[...] = total
-    tot[mine, :] = total
+    tot[chunk, :] = total
+    core = lax.rem(me, 2)
+    flip = 1 - 2 * core
     second = []
-    for d in ORDER:
+    for k, (chips, other) in enumerate(
+        ((2 * flip, 0), (2 * flip, 1), (1, 0), (1, 1), (-1, 0), (-1, 1), (0, 1))
+    ):
         copy = pltpu.make_async_remote_copy(
-            src_ref=sumt, dst_ref=tot.at[mine],
-            send_sem=s2.at[d - 1], recv_sem=r2.at[d - 1],
-            device_id={"vert": lax.rem(me + d, PEERS)}, device_id_type=MESH,
+            src_ref=sumt, dst_ref=tot.at[chunk],
+            send_sem=s2.at[k], recv_sem=r2.at[k],
+            device_id={"vert": lax.rem(me + 2 * chips + other * flip + PEERS, PEERS)}, device_id_type=MESH,
         )
         copy.start()
         second.append(copy)
 
-    send_e.wait_recv()
-    send_w.wait_recv()
-
-    def unpack_cols(v, carry):
-        rows8 = pl.ds(pl.multiple_of(v * 8, 8), 8)
-        west_in = xleft[rows8, :]
-        east_in = xright[rows8, :]
-        for n in range(HALF):
-            tile = v * HALF + n
-            right = speed_x(tile) > 0.0
-            for k in range(4):
-                at = slice(n * 4 + k, n * 4 + k + 1)
-                value = jnp.where(right, jnp.broadcast_to(west_in[:, at], (8, 128)), jnp.broadcast_to(east_in[:, at], (8, 128)))
-                edges[pl.ds(pl.multiple_of((tile * 4 + k) * 8, 8), 8), :] = value
-        return carry
-
-    lax.fori_loop(0, 2, unpack_cols, 0)
     load_w.wait()
     flags = walls_v[pl.ds(wall, 1), :].astype(F32)
     flag = jnp.broadcast_to(flags, (8, 128))
@@ -358,13 +346,10 @@
                 (inner, ci, gxi, gyi, fi, u_i),
             ):
                 f_x = c + s_x * g_x
-                at = pl.multiple_of((tile * 4 + y * 2) * 8, 8)
-                e0 = edges[pl.ds(at, 8), :]
-                e1 = edges[pl.ds(at + 8, 8), :]
                 ux0 = jnp.where(right, pltpu.roll(f_x, 1, 1), pltpu.roll(f_x, 127, 1))
                 ux2 = jnp.where(right, pltpu.roll(g_y, 1, 1), pltpu.roll(g_y, 127, 1))
-                ux0 = jnp.where(outermost, e0, ux0)
-                ux2 = jnp.where(outermost, e1, ux2)
+                ux0 = jnp.where(outermost, 0.0, ux0)
+                ux2 = jnp.where(outermost, 0.0, ux2)
                 c2 = c + c
                 mean = a_x * (f_x - ux0) + a_y * (f_y - uy0) + c2
                 rx = 3.0 * v_x * (f_x + ux0 - c2) + a_y * (g_x - uy1) + 2.0 * g_x
@@ -375,6 +360,28 @@
         return carry
 
     lax.fori_loop(0, HALF, move, 0, unroll=2)
+
+    send_e.wait_recv()
+    send_w.wait_recv()
+
+    def add_edges(v, carry):
+        rows8 = pl.ds(pl.multiple_of(v * 8, 8), 8)
+        came = jnp.where(xside[rows8, :] > 0.0, xleft[rows8, :], xright[rows8, :])
+        for n in range(HALF):
+            tile = v * HALF + n
+            speed = speed_x(tile)
+            speed = jnp.where(lane == jnp.where(speed > 0.0, 0, 127), speed, 0.0)
+            a_x = jnp.abs(speed)
+            for y in range(2):
+                value, slope = (
+                    jnp.broadcast_to(came[:, n * 4 + y * 2 + k : n * 4 + y * 2 + k + 1], (8, 128)) for k in range(2)
+                )
+                for k, term in enumerate((-a_x * value, 3.0 * speed * value, -a_x * slope)):
+                    at = pl.ds(pl.multiple_of((tile * 6 + k * 2 + y) * 8, 8), 8)
+                    tb[at, :] = tb[at, :] + term
+        return carry
+
+    lax.fori_loop(0, 2, add_edges, 0)
 
     for copy in hop2:
         copy.wait_recv()
@@ -475,10 +482,9 @@
             pltpu.VMEM((2, 128), jnp.int32),
             pltpu.VMEM((32, PAD), BF16),
             pltpu.VMEM((PAD, 256), F32),
-            pltpu.VMEM((6, 3, PAD, 256), BF16),
             pltpu.VMEM((128, 128), F32),
-            pltpu.VMEM((120, 128), F32),
-            pltpu.VMEM((8, 128), F32),
+            pltpu.VMEM((240, 128), F32),
+            pltpu.VMEM((16, 128), F32),
             pltpu.VMEM((128, 128), F32),
             pltpu.VMEM((HALF * 16, 128), F32),
             pltpu.VMEM((HALF * 16, 128), F32),
@@ -486,7 +492,7 @@
             pltpu.VMEM((16, 128), F32),
             pltpu.VMEM((16, 128), F32),
             pltpu.VMEM((16, 128), F32),
-            pltpu.VMEM((TILES * 32, 128), F32),
+            pltpu.VMEM((16, 128), F32),
             pltpu.VMEM((16 * 48, 128), F32),
             pltpu.SemaphoreType.DMA((4,)),
             pltpu.SemaphoreType.DMA((15,)),

time: 21.9 us -> 20.8 us (0.950)
  Pallas kernels: 21.8 us -> 20.7 us
    pallas_call x1, Pallas kernels: 20.4 us -> 19.2 us  [shards(): pl.pallas_call(gather, out_shape=(pltpu.VMEM((PAD_ROWS, 128), F32), pltpu...]
where the time goes in v4:
time: 20.8 us; the launch traced here: 20.7 us
  Pallas kernels  20.7 us (100%)
    pallas_call x1, Pallas kernels, shards(): pl.pallas_call(gather, out_shape=(pltpu.VMEM((PAD_ROWS, 128), F32), pltpu...  19.2 us
    pallas_call x1, Pallas kernels, shards(): pl.pallas_call(collide, out_shape=jax.ShapeDtypeStruct((ROWS, 128), F32),...  1.48 us

profile of v4, /device:TPU:1, one launch (start us, length us, event | category | flops | bytes accessed | tf_op | source)
XLA Modules:
  0.0 20.7 jit_solution(1088995524696962488)
XLA Ops:
  0.0 19.2 %shard_map.46 = (f32[3072,128]{1,0:T(8,128)S(1)}, bf16[512,128]{1,0:T(8,128)(2,1)S(1)}, bf16[8,128,256]{2,1,0:T(8,128)(2,1)S(1)}) custom-call(f32[3000,128]{1,0:T(8,128)} %bitcast.4, f32[3000,128]{1,0:T(8,128)} %bitcast.5, s32[2,500]{1,0:T(2,128)} %bitcast.6, s32[2,128]{1,0:T(2,128)} %walls_hbm.1), custom_call_target="tpu_custom_call" | custom-call | tf_op jit(solution)/shard_map/pallas_call | solution.py:468
  19.2 1.5 %shard_map.47 = f32[3000,128]{1,0:T(8,128)} custom-call(f32[3072,128]{1,0:T(8,128)S(1)} %get-tuple-element.8.tb, bf16[512,128]{1,0:T(8,128)(2,1)S(1)} %get-tuple-element.9.mg, bf16[8,128,256]{2,1,0:T(8,128)(2,1)S(1)} %get-tuple-element.10.csb), custom_call_target="tpu_custom_call" | custom-call | tf_op jit(solution)/shard_map/pallas_call | solution.py:515

commit v5 on v4

--- a/solution.py
+++ b/solution.py
@@ -104,13 +104,20 @@
     gy = lax.axis_index("gy")
     wall = gy
     inner = 1 - gy
-    load_t = pltpu.make_async_copy(tan_hbm, xt.at[pl.ds(0, ROWS)], lsem.at[0])
-    load_s = pltpu.make_async_copy(state_hbm, xs.at[pl.ds(0, ROWS)], lsem.at[1])
-    load_o = pltpu.make_async_copy(orient_hbm, orient_v, lsem.at[2])
-    load_w = pltpu.make_async_copy(walls_hbm, walls_v, lsem.at[3])
+    load_t, load_s = (
+        [
+            pltpu.make_async_copy(
+                hbm.at[pl.ds(k * 1536, size)], ref.at[pl.ds(k * 1536, size)], lsem.at[2 * n + k]
+            )
+            for k, size in enumerate((1536, ROWS - 1536))
+        ]
+        for n, (hbm, ref) in enumerate(((tan_hbm, xt), (state_hbm, xs)))
+    )
+    load_o = pltpu.make_async_copy(orient_hbm, orient_v, lsem.at[4])
+    load_w = pltpu.make_async_copy(walls_hbm, walls_v, lsem.at[5])
     load_o.start()
-    load_t.start()
-    load_s.start()
+    for copy in load_t + load_s:
+        copy.start()
     load_w.start()
 
     barrier = pltpu.get_barrier_semaphore()
@@ -183,7 +190,29 @@
     def speed_y(tile):
         return vxy[pl.ds(pl.multiple_of(tile * 8, 8), 8), 128:256]
 
-    load_t.wait()
+
+    group = sub // 2
+    packed = [None] * 3
+
+    def sums(ref, first, loads):
+        accs = [None] * 3
+        for k in range(2):
+            loads[k].wait()
+            for p in range(3):
+                pair = [ref[pl.ds(k * 1536 + 2 * p + h, 256, stride=6), :] for h in range(2)]
+                for piece in split3(jnp.concatenate(pair, axis=1)):
+                    got = jnp.dot(ml[:, k * 256 : k * 256 + 256], piece.astype(BF16), preferred_element_type=F32)
+                    accs[p] = got if accs[p] is None else accs[p] + got
+        for p, acc in enumerate(accs):
+            for h in range(2):
+                c = first + 2 * p + h
+                cols = slice(h * 128, h * 128 + 128)
+                part[pl.ds(c * 8, 8), :] = acc[0:8, cols] + acc[8:16, cols]
+                extra = acc[16:24, cols] + acc[24:32, cols]
+                old = packed[c // 4]
+                packed[c // 4] = extra if old is None else jnp.where(group == c % 4, extra, old)
+
+    sums(xt, 6, load_t)
 
     def pack_rows(t, carry):
         traces = []
@@ -200,33 +229,27 @@
 
     lax.fori_loop(0, HALF, pack_rows, 0, unroll=4)
 
-    group = sub // 2
-    packed = [None] * 3
-
-    def sums(ref, first):
-        for p in range(3):
-            acc = None
-            for k in range(2):
-                pair = [ref[pl.ds(k * 1536 + 2 * p + h, 256, stride=6), :] for h in range(2)]
-                for piece in split3(jnp.concatenate(pair, axis=1)):
-                    got = jnp.dot(ml[:, k * 256 : k * 256 + 256], piece.astype(BF16), preferred_element_type=F32)
-                    acc = got if acc is None else acc + got
-            for h in range(2):
-                c = first + 2 * p + h
-                cols = slice(h * 128, h * 128 + 128)
-                part[pl.ds(c * 8, 8), :] = acc[0:8, cols] + acc[8:16, cols]
-                extra = acc[16:24, cols] + acc[24:32, cols]
-                old = packed[c // 4]
-                packed[c // 4] = extra if old is None else jnp.where(group == c % 4, extra, old)
-
-    sums(xt, 6)
-    load_s.wait()
-    sums(xs, 0)
+    sums(xs, 0, load_s)
     for i in range(3):
         part[pl.ds((12 + i) * 8, 8), :] = packed[i]
     part[pl.ds(120, 8), :] = jnp.zeros((8, 128), F32)
 
     pl.semaphore_wait(barrier, PEERS + 2)
+
+    hop1 = []
+    hop2 = []
+    for n, to in enumerate((plus, minus, plus, minus)):
+        piece = pl.ds(n * HALF * 4, HALF * 4)
+        hop1.append(pltpu.make_async_remote_copy(
+            src_ref=vsend.at[piece], dst_ref=relay.at[piece], send_sem=ysem.at[0, n], recv_sem=ysem.at[1, n],
+            device_id=to, device_id_type=MESH,
+        ))
+        hop2.append(pltpu.make_async_remote_copy(
+            src_ref=relay.at[piece], dst_ref=vrecv.at[piece], send_sem=ysem.at[2, n], recv_sem=ysem.at[3, n],
+            device_id=to, device_id_type=MESH,
+        ))
+    for copy in hop1:
+        copy.start()
 
     first = []
     for d in ORDER:
@@ -240,23 +263,6 @@
         copy.start()
         first.append(copy)
 
-    halves = (pl.ds(0, HALF * 8), pl.ds(HALF * 8, HALF * 8))
-    hop1 = [
-        pltpu.make_async_remote_copy(
-            src_ref=vsend.at[halves[n]], dst_ref=relay.at[halves[n]], send_sem=ysem.at[0, n], recv_sem=ysem.at[1, n],
-            device_id=to, device_id_type=MESH,
-        )
-        for n, to in enumerate((plus, minus))
-    ]
-    hop2 = [
-        pltpu.make_async_remote_copy(
-            src_ref=relay.at[halves[n]], dst_ref=vrecv.at[halves[n]], send_sem=ysem.at[2, n], recv_sem=ysem.at[3, n],
-            device_id=to, device_id_type=MESH,
-        )
-        for n, to in enumerate((plus, minus))
-    ]
-    for copy in hop1:
-        copy.start()
 
     quad_lane = lane >> 2
 
@@ -291,9 +297,9 @@
     send_e.start()
     send_w.start()
 
-    for came, goes in zip(hop1, hop2):
-        came.wait_recv()
-        goes.start()
+    for n in range(2):
+        hop1[n].wait_recv()
+        hop2[n].start()
 
     for copy in first:
         copy.wait_recv()
@@ -316,6 +322,10 @@
         )
         copy.start()
         second.append(copy)
+
+    for n in range(2, 4):
+        hop1[n].wait_recv()
+        hop2[n].start()
 
     load_w.wait()
     flags = walls_v[pl.ds(wall, 1), :].astype(F32)
@@ -383,6 +393,33 @@
 
     lax.fori_loop(0, 2, add_edges, 0)
 
+    for copy in second:
+        copy.wait_recv()
+    upper = sub >= 4
+    q_of = lax.rem(sub, 4)
+    xi = jnp.where(q_of >= 2, GAUSS, -GAUSS)
+    eta = jnp.where(lax.rem(q_of, 2) == 1, GAUSS, -GAUSS)
+
+    def moment(k):
+        s, n = divmod(k, 10)
+        coefs = []
+        for j in range(6):
+            c = s * 6 + j
+            at = c * 8 + n if n < 8 else (12 + c // 4) * 8 + (c % 4) * 2 + n - 8
+            coefs.append(jnp.broadcast_to(tot[pl.ds(at, 1), :], (8, 128)))
+        a, b, c = (jnp.where(upper, coefs[2 * m + 1], coefs[2 * m]) for m in range(3))
+        return a + xi * b + eta * c
+
+    expo, fact = gauss_coefs([moment(k) for k in range(20)])
+    for half, coefs in enumerate((expo, fact)):
+        for k, x in enumerate(coefs):
+            for n, piece in enumerate(split3(x)):
+                for r in (k,) if k < 4 else (k, k + 6):
+                    cs[pl.ds(half * 384 + n * 16 + r, 8, stride=48), :] = piece
+    for i in range(8):
+        csb[i, 0:48, 0:128] = cs[i * 48 : i * 48 + 48, :].astype(BF16)
+        csb[i, 0:48, 128:256] = cs[384 + i * 48 : 384 + i * 48 + 48, :].astype(BF16)
+
     for copy in hop2:
         copy.wait_recv()
 
@@ -402,32 +439,6 @@
 
     lax.fori_loop(0, HALF, add_halo, 0, unroll=4)
 
-    for copy in second:
-        copy.wait_recv()
-    upper = sub >= 4
-    q_of = lax.rem(sub, 4)
-    xi = jnp.where(q_of >= 2, GAUSS, -GAUSS)
-    eta = jnp.where(lax.rem(q_of, 2) == 1, GAUSS, -GAUSS)
-
-    def moment(k):
-        s, n = divmod(k, 10)
-        coefs = []
-        for j in range(6):
-            c = s * 6 + j
-            at = c * 8 + n if n < 8 else (12 + c // 4) * 8 + (c % 4) * 2 + n - 8
-            coefs.append(jnp.broadcast_to(tot[pl.ds(at, 1), :], (8, 128)))
-        a, b, c = (jnp.where(upper, coefs[2 * m + 1], coefs[2 * m]) for m in range(3))
-        return a + xi * b + eta * c
-
-    expo, fact = gauss_coefs([moment(k) for k in range(20)])
-    for half, coefs in enumerate((expo, fact)):
-        for k, x in enumerate(coefs):
-            for n, piece in enumerate(split3(x)):
-                for r in (k,) if k < 4 else (k, k + 6):
-                    cs[pl.ds(half * 384 + n * 16 + r, 8, stride=48), :] = piece
-    for i in range(8):
-        csb[i, 0:48, 0:128] = cs[i * 48 : i * 48 + 48, :].astype(BF16)
-        csb[i, 0:48, 128:256] = cs[384 + i * 48 : 384 + i * 48 + 48, :].astype(BF16)
     for copy in first + second + hop1 + hop2 + [send_e, send_w]:
         copy.wait_send()
 
@@ -438,7 +449,7 @@
     for n in range(PARTS):
         rows = slice(n * tiles * 8, (n + 1) * tiles * 8)
         for i in range(8):
-            eq[i, rows, :] = jnp.dot(mg[rows, :], csb[i], preferred_element_type=F32)
+            eq[i, rows, :] = jnp.dot(mg[rows, 0:48], csb[i, 0:48, :], preferred_element_type=F32)
         for t in range(n * tiles, (n + 1) * tiles):
             rows8 = slice(t * 8, t * 8 + 8)
             for y in range(2):
@@ -494,12 +505,12 @@
             pltpu.VMEM((16, 128), F32),
             pltpu.VMEM((16, 128), F32),
             pltpu.VMEM((16 * 48, 128), F32),
-            pltpu.SemaphoreType.DMA((4,)),
+            pltpu.SemaphoreType.DMA((6,)),
             pltpu.SemaphoreType.DMA((15,)),
             pltpu.SemaphoreType.DMA((15,)),
             pltpu.SemaphoreType.DMA((15,)),
             pltpu.SemaphoreType.DMA((15,)),
-            pltpu.SemaphoreType.DMA((4, 2)),
+            pltpu.SemaphoreType.DMA((4, 4)),
             pltpu.SemaphoreType.DMA((2,)),
             pltpu.SemaphoreType.DMA((2,)),
         ],

time: 20.8 us -> 20.4 us (0.981)
  Pallas kernels: 20.7 us -> 20.3 us
    pallas_call x1, Pallas kernels: 19.2 us -> 18.9 us  [shards(): pl.pallas_call(gather, out_shape=(pltpu.VMEM((PAD_ROWS, 128), F32), pltpu...]
where the time goes in v5:
time: 20.4 us; the launch traced here: 20.3 us
  Pallas kernels  20.3 us (100%)
    pallas_call x1, Pallas kernels, shards(): pl.pallas_call(gather, out_shape=(pltpu.VMEM((PAD_ROWS, 128), F32), pltpu...  18.9 us
    pallas_call x1, Pallas kernels, shards(): pl.pallas_call(collide, out_shape=jax.ShapeDtypeStruct((ROWS, 128), F32),...  1.47 us

profile of v5, /device:TPU:1, one launch (start us, length us, event | category | flops | bytes accessed | tf_op | source)
XLA Modules:
  0.0 20.3 jit_solution(5475739042856849080)
XLA Ops:
  0.0 18.9 %shard_map.46 = (f32[3072,128]{1,0:T(8,128)S(1)}, bf16[512,128]{1,0:T(8,128)(2,1)S(1)}, bf16[8,128,256]{2,1,0:T(8,128)(2,1)S(1)}) custom-call(f32[3000,128]{1,0:T(8,128)} %bitcast.4, f32[3000,128]{1,0:T(8,128)} %bitcast.5, s32[2,500]{1,0:T(2,128)} %bitcast.6, s32[2,128]{1,0:T(2,128)} %walls_hbm.1), custom_call_target="tpu_custom_call" | custom-call | tf_op jit(solution)/shard_map/pallas_call | solution.py:479
  18.9 1.5 %shard_map.47 = f32[3000,128]{1,0:T(8,128)} custom-call(f32[3072,128]{1,0:T(8,128)S(1)} %get-tuple-element.8.tb, bf16[512,128]{1,0:T(8,128)(2,1)S(1)} %get-tuple-element.9.mg, bf16[8,128,256]{2,1,0:T(8,128)(2,1)S(1)} %get-tuple-element.10.csb), custom_call_target="tpu_custom_call" | custom-call | tf_op jit(solution)/shard_map/pallas_call | solution.py:526

commit v6 on v5

--- a/solution.py
+++ b/solution.py
@@ -238,8 +238,10 @@
 
     hop1 = []
     hop2 = []
-    for n, to in enumerate((plus, minus, plus, minus)):
-        piece = pl.ds(n * HALF * 4, HALF * 4)
+    for n, (to, begin, size) in enumerate(
+        ((plus, 0, 192), (minus, 192, 192), (plus, 384, 64), (minus, 448, 64))
+    ):
+        piece = pl.ds(begin, size)
         hop1.append(pltpu.make_async_remote_copy(
             src_ref=vsend.at[piece], dst_ref=relay.at[piece], send_sem=ysem.at[0, n], recv_sem=ysem.at[1, n],
             device_id=to, device_id_type=MESH,

time: 20.4 us -> 20.4 us (level)
  no operation moved by 1% of the time
where the time goes in v6:
time: 20.4 us; the launch traced here: 20.3 us
  Pallas kernels  20.3 us (100%)
    pallas_call x1, Pallas kernels, shards(): pl.pallas_call(gather, out_shape=(pltpu.VMEM((PAD_ROWS, 128), F32), pltpu...  18.9 us
    pallas_call x1, Pallas kernels, shards(): pl.pallas_call(collide, out_shape=jax.ShapeDtypeStruct((ROWS, 128), F32),...  1.47 us

profile of v6, /device:TPU:1, one launch (start us, length us, event | category | flops | bytes accessed | tf_op | source)
XLA Modules:
  0.0 20.3 jit_solution(6771773771642229211)
XLA Ops:
  0.0 18.9 %shard_map.46 = (f32[3072,128]{1,0:T(8,128)S(1)}, bf16[512,128]{1,0:T(8,128)(2,1)S(1)}, bf16[8,128,256]{2,1,0:T(8,128)(2,1)S(1)}) custom-call(f32[3000,128]{1,0:T(8,128)} %bitcast.4, f32[3000,128]{1,0:T(8,128)} %bitcast.5, s32[2,500]{1,0:T(2,128)} %bitcast.6, s32[2,128]{1,0:T(2,128)} %walls_hbm.1), custom_call_target="tpu_custom_call" | custom-call | tf_op jit(solution)/shard_map/pallas_call | solution.py:481
  18.9 1.5 %shard_map.47 = f32[3000,128]{1,0:T(8,128)} custom-call(f32[3072,128]{1,0:T(8,128)S(1)} %get-tuple-element.8.tb, bf16[512,128]{1,0:T(8,128)(2,1)S(1)} %get-tuple-element.9.mg, bf16[8,128,256]{2,1,0:T(8,128)(2,1)S(1)} %get-tuple-element.10.csb), custom_call_target="tpu_custom_call" | custom-call | tf_op jit(solution)/shard_map/pallas_call | solution.py:528
